TPU v7x, 32 devices: a whole 2x2x4 slice. The times are simulated.
32 devices in a mesh: dp: 8 (over z, x), tensor: 4 (over y, core).
Axes of the slice: x: 2, y: 2, z: 4, core: 2. Of those that a mesh axis runs over, the one named last changes fastest.
Arguments:
- inputs: bfloat16 [8, 1024, 2048], P('dp'), may hold values from -6 to 6
- lengths: int32 [8], P('dp'), may hold values from 256 to 1024, as said below
- loss_mask: int32 [8, 1024], P('dp'), may hold values 0 or 1
- teacher: bfloat16 [8, 1024, 2048], P('dp'), may hold values from -6 to 6
- attn_gain: bfloat16 [2048], P('dp'), may hold values from 0.5 to 1.5
- q_weight: bfloat16 [2048, 2048], P('dp', 'tensor'), may hold values from -0.125 to 0.125
- k_weight: bfloat16 [2048, 2048], P('dp', 'tensor'), may hold values from -0.125 to 0.125
- v_weight: bfloat16 [2048, 4096], P('dp', 'tensor'), may hold values from -0.125 to 0.125
- gating_weight: bfloat16 [2048, 4096], P('dp', 'tensor'), may hold values from -0.125 to 0.125
- alpha_weight: bfloat16 [2048, 16], P('dp', 'tensor'), may hold values from -0.125 to 0.125
- beta_weight: bfloat16 [2048, 16], P('dp', 'tensor'), may hold values from -0.125 to 0.125
- q_conv: float32 [4, 2048], P(None, 'tensor'), may hold values from -3 to 3
- k_conv: float32 [4, 2048], P(None, 'tensor'), may hold values from -3 to 3
- v_conv: float32 [4, 4096], P(None, 'tensor'), may hold values from -3 to 3
- decay_log: float32 [16], P('tensor'), may hold values from -1 to 0.5
- decay_bias: float32 [16], P('tensor'), may hold values from -6 to -1
- out_gain: float32 [256], replicated, may hold values from 0.5 to 1.5
- out_weight: bfloat16 [4096, 2048], P('tensor', 'dp'), may hold values from -0.1875 to 0.1875
- ffn_gain: bfloat16 [2048], P('dp'), may hold values from 0.5 to 1.5
- ffn_gate: bfloat16 [2048, 5632], P('dp', 'tensor'), may hold values from -0.125 to 0.125
- ffn_up: bfloat16 [2048, 5632], P('dp', 'tensor'), may hold values from -0.125 to 0.125
- ffn_down: bfloat16 [5632, 2048], P('tensor', 'dp'), may hold values from -0.15625 to 0.15625
Outputs:
- activations: bfloat16 [8, 1024, 2048], P('dp', 'tensor')
- loss: float32 [], replicated
- input_grad: float32 [8, 1024, 2048], P('dp', 'tensor')
- attn_gain_grad: float32 [2048], P('dp')
- q_weight_grad: float32 [2048, 2048], P('dp', 'tensor')
- k_weight_grad: float32 [2048, 2048], P('dp', 'tensor')
- v_weight_grad: float32 [2048, 4096], P('dp', 'tensor')
- gating_weight_grad: float32 [2048, 4096], P('dp', 'tensor')
- alpha_weight_grad: float32 [2048, 16], P('dp', 'tensor')
- beta_weight_grad: float32 [2048, 16], P('dp', 'tensor')
- q_conv_grad: float32 [4, 2048], P(None, 'tensor')
- k_conv_grad: float32 [4, 2048], P(None, 'tensor')
- v_conv_grad: float32 [4, 4096], P(None, 'tensor')
- decay_log_grad: float32 [16], P('tensor')
- decay_bias_grad: float32 [16], P('tensor')
- out_gain_grad: float32 [256], replicated
- out_weight_grad: float32 [4096, 2048], P('tensor', 'dp')
- ffn_gain_grad: float32 [2048], P('dp')
- ffn_gate_grad: float32 [2048, 5632], P('dp', 'tensor')
- ffn_up_grad: float32 [2048, 5632], P('dp', 'tensor')
- ffn_down_grad: float32 [5632, 2048], P('tensor', 'dp')
Inputs may be any that keep to these rules, and one draw needn't show every extreme that they name: A sequence's valid tokens are its first lengths slots; in every draw one sequence has 1024 and another 256.
All inputs are finite; a program needn't handle non-finite values. No bound on the sum of `loss_mask` on one device may be relied on, other than what follows from the above.
Results may differ from a plain program's by a relative error of at most 0.018.
Values may be sent and summed in bfloat16 or wider, within the bound.
A program may use at most 320 MiB of HBM per device.

v0:
```python
import jax
import jax.numpy as jnp
from jax import lax
from jax.sharding import PartitionSpec as P

SPAN = 64


def causal_conv(values, kernel):
    kernel_len = kernel.shape[0]
    length = values.shape[1]
    padded = jnp.pad(values, ((0, 0), (kernel_len - 1, 0), (0, 0)))
    summed = padded[:, 0:length, :] * kernel[0]
    for offset in range(1, kernel_len):
        summed = summed + padded[:, offset : offset + length, :] * kernel[offset]
    return jax.nn.silu(summed)


def unit_rows(values):
    return values * lax.rsqrt(jnp.sum(values * values, -1, keepdims=True) + 1e-06)


def to_blocks(values, block_len):
    batch_n = values.shape[0]
    count_n = values.shape[1] // block_len
    shaped = values.reshape((batch_n, count_n, block_len) + values.shape[2:])
    if values.ndim == 4:
        return shaped.transpose(1, 0, 3, 2, 4)
    return shaped.transpose(1, 0, 3, 2)


def delta_block(memory, block):
    queries, key_rows, values, beta_val, decays = block
    block_len = decays.shape[-1]
    highest = lax.Precision.HIGHEST
    cumulative = jnp.cumsum(decays, -1)
    spread = cumulative[..., :, None] - cumulative[..., None, :]
    row_index = lax.broadcasted_iota(jnp.int32, (block_len, block_len), 0)
    col_index = lax.broadcasted_iota(jnp.int32, (block_len, block_len), 1)
    strict = row_index > col_index
    within = row_index >= col_index
    key_decay = jnp.exp(jnp.where(strict, spread, 0.0)) * strict.astype(jnp.float32)
    key_mix = (
        jnp.einsum("bhid,bhjd->bhij", key_rows * beta_val[..., None], key_rows, precision=highest)
        * key_decay
    )
    identity = jnp.eye(block_len, dtype=decays.dtype)
    right_side = jnp.concatenate(
        [key_rows * (beta_val * jnp.exp(cumulative))[..., None], values * beta_val[..., None]], -1
    )
    solved = jax.scipy.linalg.solve_triangular(
        identity + key_mix, right_side, lower=True, unit_diagonal=True
    )
    key_dim = key_rows.shape[-1]
    fresh_vals = solved[..., key_dim:] - jnp.einsum(
        "bhcd,bhde->bhce", solved[..., :key_dim], memory, precision=highest
    )
    query_decay = jnp.exp(jnp.where(within, spread, 0.0)) * within.astype(jnp.float32)
    scores = jnp.einsum("bhid,bhjd->bhij", queries, key_rows, precision=highest) * query_decay
    result = jnp.einsum(
        "bhcd,bhde->bhce", queries * jnp.exp(cumulative)[..., None], memory, precision=highest
    )
    result = result + jnp.einsum("bhij,bhje->bhie", scores, fresh_vals, precision=highest)
    final_sum = cumulative[..., -1]
    carried = jnp.exp(final_sum)[..., None, None] * memory + jnp.einsum(
        "bhcd,bhce->bhde",
        key_rows * jnp.exp(final_sum[..., None] - cumulative)[..., None],
        fresh_vals,
        precision=highest,
    )
    return (carried, result)


def mixer(
    q_proj,
    k_proj,
    v_proj,
    g_proj,
    a_proj,
    b_proj,
    q_kernel,
    k_kernel,
    v_kernel,
    decay_log,
    decay_bias,
    out_gain,
):
    batch_n, length, head_n = a_proj.shape
    queries = unit_rows(causal_conv(q_proj, q_kernel).reshape(batch_n, length, head_n, -1))
    queries = queries * queries.shape[-1] ** (-0.5)
    key_rows = unit_rows(causal_conv(k_proj, k_kernel).reshape(batch_n, length, head_n, -1))
    values = causal_conv(v_proj, v_kernel).reshape(batch_n, length, head_n, -1)
    beta_val = jax.nn.sigmoid(b_proj)
    decays = -jnp.exp(decay_log) * jax.nn.softplus(a_proj + decay_bias)
    memory = jnp.zeros((batch_n, head_n, key_rows.shape[-1], values.shape[-1]), jnp.float32)
    blocks = (
        to_blocks(queries, SPAN),
        to_blocks(key_rows, SPAN),
        to_blocks(values, SPAN),
        to_blocks(beta_val, SPAN),
        to_blocks(decays, SPAN),
    )
    memory, outputs = lax.scan(jax.checkpoint(delta_block), memory, blocks)
    merged = outputs.transpose(1, 0, 3, 2, 4).reshape(batch_n, length, head_n, -1)
    gating = g_proj.reshape(batch_n, length, head_n, -1)
    normed = (
        merged
        * lax.rsqrt(jnp.mean(merged * merged, -1, keepdims=True) + 1e-05)
        * out_gain
        * jax.nn.silu(gating)
    )
    return normed.reshape(batch_n, length, -1)


def norm_back(values, rms_inv, gain, d_normed):
    scaled = d_normed * gain
    gain_grad = jnp.sum(d_normed * values * rms_inv, 0)
    d_values = rms_inv * scaled - values * rms_inv**3 * jnp.mean(scaled * values, -1, keepdims=True)
    return (d_values, gain_grad)


def weight_grad(source, d_target):
    return jnp.einsum("td,te->de", source, d_target, preferred_element_type=jnp.float32)


def back_product(d_target, weight):
    return jnp.einsum("te,de->td", d_target, weight, preferred_element_type=jnp.float32)


def body(
    inputs,
    lengths,
    loss_mask,
    teacher,
    attn_gain,
    q_weight,
    k_weight,
    v_weight,
    gating_weight,
    alpha_weight,
    beta_weight,
    q_conv,
    k_conv,
    v_conv,
    decay_log,
    decay_bias,
    out_gain,
    out_weight,
    ffn_gain,
    ffn_gate,
    ffn_up,
    ffn_down,
):
    seq_count, slot_n, width_n = inputs.shape
    tokens_n = seq_count * slot_n
    share_n = slot_n // lax.axis_size("tensor")
    share_start = lax.axis_index("tensor") * share_n
    share_rows = seq_count * share_n
    positions = lax.broadcasted_iota(jnp.int32, (seq_count, slot_n), 1)
    valid = (positions < lengths[:, None]).astype(jnp.float32)
    tok_weight = valid * loss_mask.astype(jnp.float32)
    gathered = (
        lax.all_gather(attn_gain, "dp", axis=0, tiled=True),
        lax.all_gather(q_weight, "dp", axis=0, tiled=True),
        lax.all_gather(k_weight, "dp", axis=0, tiled=True),
        lax.all_gather(v_weight, "dp", axis=0, tiled=True),
        lax.all_gather(gating_weight, "dp", axis=0, tiled=True),
        lax.all_gather(alpha_weight, "dp", axis=0, tiled=True),
        lax.all_gather(beta_weight, "dp", axis=0, tiled=True),
        lax.all_gather(out_weight, "dp", axis=1, tiled=True),
        lax.all_gather(ffn_gain, "dp", axis=0, tiled=True),
        lax.all_gather(ffn_gate, "dp", axis=0, tiled=True),
        lax.all_gather(ffn_up, "dp", axis=0, tiled=True),
        lax.all_gather(ffn_down, "dp", axis=1, tiled=True),
    )
    (
        gain_attn,
        query_w,
        key_w,
        value_w,
        gating_w,
        alpha_w,
        beta_w,
        out_w,
        gain_ffn,
        gate_w,
        up_w,
        down_w,
    ) = gathered
    gain_attn = gain_attn.astype(jnp.float32)
    gain_ffn = gain_ffn.astype(jnp.float32)
    flat_in = inputs.reshape(tokens_n, width_n).astype(jnp.float32)
    attn_rms = lax.rsqrt(jnp.mean(flat_in * flat_in, -1, keepdims=True) + 1e-06)
    normed = (flat_in * attn_rms * gain_attn).astype(jnp.bfloat16)

    def project(weight):
        return jnp.dot(normed, weight, preferred_element_type=jnp.float32).reshape(
            seq_count, slot_n, -1
        )

    mixed_out, mixer_back = jax.vjp(
        mixer,
        project(query_w),
        project(key_w),
        project(value_w),
        project(gating_w),
        project(alpha_w),
        project(beta_w),
        q_conv,
        k_conv,
        v_conv,
        decay_log,
        decay_bias,
        out_gain,
    )
    mixed_low = mixed_out.reshape(tokens_n, -1).astype(jnp.bfloat16)
    attn_part = jnp.dot(mixed_low, out_w, preferred_element_type=jnp.float32)

    def share_of(array):
        return lax.dynamic_slice_in_dim(array, share_start, share_n, 1)

    attn_own = lax.psum_scatter(
        attn_part.reshape(seq_count, slot_n, width_n), "tensor", scatter_dimension=1, tiled=True
    )
    base_in = share_of(inputs).reshape(share_rows, width_n).astype(jnp.float32)
    base_rms = lax.rsqrt(jnp.mean(base_in * base_in, -1, keepdims=True) + 1e-06)
    row_weight = share_of(tok_weight).reshape(share_rows, 1)
    row_valid = share_of(valid).reshape(share_rows, 1)
    row_teacher = share_of(teacher).reshape(share_rows, width_n).astype(jnp.float32)
    resid = base_in + attn_own.reshape(share_rows, width_n)
    ffn_rms = lax.rsqrt(jnp.mean(resid * resid, -1, keepdims=True) + 1e-06)
    normed_own = (
        (resid * ffn_rms * gain_ffn).astype(jnp.bfloat16).reshape(seq_count, share_n, width_n)
    )
    normed_ffn = lax.all_gather(normed_own, "tensor", axis=1, tiled=True).reshape(tokens_n, width_n)
    gate_pre = jnp.dot(normed_ffn, gate_w, preferred_element_type=jnp.float32)
    up_pre = jnp.dot(normed_ffn, up_w, preferred_element_type=jnp.float32)
    sig_gate = jax.nn.sigmoid(gate_pre)
    silu_gate = gate_pre * sig_gate
    hidden = (silu_gate * up_pre).astype(jnp.bfloat16)
    ffn_part = jnp.dot(hidden, down_w, preferred_element_type=jnp.float32)
    ffn_own = lax.psum_scatter(
        ffn_part.reshape(seq_count, slot_n, width_n), "tensor", scatter_dimension=1, tiled=True
    )
    output = resid + ffn_own.reshape(share_rows, width_n)
    error = (output - row_teacher) * row_weight
    error_all, count_all = lax.psum((jnp.sum(error * error), jnp.sum(row_weight)), ("dp", "tensor"))
    loss = error_all / count_all
    coef = 0.5 * tokens_n * lax.axis_size("dp") / count_all
    d_output = 2.0 * coef * error * row_weight
    again = (
        lax.all_gather(attn_gain, "dp", axis=0, tiled=True),
        lax.all_gather(q_weight, "dp", axis=0, tiled=True),
        lax.all_gather(k_weight, "dp", axis=0, tiled=True),
        lax.all_gather(v_weight, "dp", axis=0, tiled=True),
        lax.all_gather(gating_weight, "dp", axis=0, tiled=True),
        lax.all_gather(alpha_weight, "dp", axis=0, tiled=True),
        lax.all_gather(beta_weight, "dp", axis=0, tiled=True),
        lax.all_gather(out_weight, "dp", axis=1, tiled=True),
        lax.all_gather(ffn_gain, "dp", axis=0, tiled=True),
        lax.all_gather(ffn_gate, "dp", axis=0, tiled=True),
        lax.all_gather(ffn_up, "dp", axis=0, tiled=True),
        lax.all_gather(ffn_down, "dp", axis=1, tiled=True),
    )
    (
        back_gain_attn,
        back_query,
        back_key,
        back_value,
        back_gating,
        back_alpha,
        back_beta,
        back_out,
        back_gain_ffn,
        back_gate,
        back_up,
        back_down,
    ) = again
    back_gain_attn = back_gain_attn.astype(jnp.float32)
    back_gain_ffn = back_gain_ffn.astype(jnp.float32)
    d_ffn_own = d_output.astype(jnp.bfloat16).reshape(seq_count, share_n, width_n)
    d_ffn = lax.all_gather(d_ffn_own, "tensor", axis=1, tiled=True).reshape(tokens_n, width_n)
    down_grad = weight_grad(hidden, d_ffn)
    d_hidden = back_product(d_ffn, back_down)
    d_gate = (d_hidden * up_pre * sig_gate * (1.0 + gate_pre * (1.0 - sig_gate))).astype(
        jnp.bfloat16
    )
    d_up = (d_hidden * silu_gate).astype(jnp.bfloat16)
    gate_grad = weight_grad(normed_ffn, d_gate)
    up_grad = weight_grad(normed_ffn, d_up)
    d_nffn_part = back_product(d_gate, back_gate) + back_product(d_up, back_up)
    d_nffn = (
        lax.psum_scatter(
            d_nffn_part.reshape(seq_count, slot_n, width_n).astype(jnp.bfloat16),
            "tensor",
            scatter_dimension=1,
            tiled=True,
        )
        .astype(jnp.float32)
        .reshape(share_rows, width_n)
    )
    d_resid_norm, ffn_gain_grad = norm_back(resid, ffn_rms, back_gain_ffn, d_nffn)
    d_resid = d_output + d_resid_norm
    d_attn_own = d_resid.astype(jnp.bfloat16).reshape(seq_count, share_n, width_n)
    d_attn = lax.all_gather(d_attn_own, "tensor", axis=1, tiled=True).reshape(tokens_n, width_n)
    out_grad = weight_grad(mixed_low, d_attn)
    d_mixed = back_product(d_attn, back_out).reshape(seq_count, slot_n, -1)
    (
        d_query,
        d_key,
        d_value,
        d_gating,
        d_alpha,
        d_beta,
        q_conv_grad,
        k_conv_grad,
        v_conv_grad,
        decay_log_part,
        decay_bias_part,
        out_gain_part,
    ) = mixer_back(d_mixed)
    d_query = d_query.reshape(tokens_n, -1).astype(jnp.bfloat16)
    d_key = d_key.reshape(tokens_n, -1).astype(jnp.bfloat16)
    d_value = d_value.reshape(tokens_n, -1).astype(jnp.bfloat16)
    d_gating = d_gating.reshape(tokens_n, -1).astype(jnp.bfloat16)
    d_alpha = d_alpha.reshape(tokens_n, -1).astype(jnp.bfloat16)
    d_beta = d_beta.reshape(tokens_n, -1).astype(jnp.bfloat16)
    query_grad = weight_grad(normed, d_query)
    key_grad = weight_grad(normed, d_key)
    value_grad = weight_grad(normed, d_value)
    gating_grad = weight_grad(normed, d_gating)
    alpha_grad = weight_grad(normed, d_alpha)
    beta_grad = weight_grad(normed, d_beta)
    d_norm_part = (
        back_product(d_query, back_query)
        + back_product(d_key, back_key)
        + back_product(d_value, back_value)
        + back_product(d_gating, back_gating)
        + back_product(d_alpha, back_alpha)
        + back_product(d_beta, back_beta)
    )
    gain_len = width_n // lax.axis_size("dp")
    gain_start = lax.axis_index("dp") * gain_len
    d_norm = (
        lax.psum_scatter(
            d_norm_part.reshape(seq_count, slot_n, width_n).astype(jnp.bfloat16),
            "tensor",
            scatter_dimension=1,
            tiled=True,
        )
        .astype(jnp.float32)
        .reshape(share_rows, width_n)
    )
    d_in_norm, attn_gain_grad = norm_back(base_in, base_rms, back_gain_attn, d_norm)
    input_rows = d_resid + d_in_norm
    attn_gain_sum, ffn_gain_sum, out_gain_sum = lax.psum(
        (attn_gain_grad, ffn_gain_grad, out_gain_part), ("dp", "tensor")
    )
    small_sums = (
        lax.psum(q_conv_grad.astype(jnp.bfloat16), "dp").astype(jnp.float32),
        lax.psum(k_conv_grad.astype(jnp.bfloat16), "dp").astype(jnp.float32),
        lax.psum(v_conv_grad.astype(jnp.bfloat16), "dp").astype(jnp.float32),
        lax.psum(decay_log_part.astype(jnp.bfloat16), "dp").astype(jnp.float32),
        lax.psum(decay_bias_part.astype(jnp.bfloat16), "dp").astype(jnp.float32),
    )
    q_conv_sum, k_conv_sum, v_conv_sum, decay_log_sum, decay_bias_sum = small_sums
    input_grad = input_rows.reshape(seq_count, share_n, width_n)
    activations = (output * row_valid).astype(jnp.bfloat16).reshape(seq_count, share_n, width_n)
    attn_gain_out = lax.dynamic_slice_in_dim(attn_gain_sum, gain_start, gain_len, 0)
    ffn_gain_out = lax.dynamic_slice_in_dim(ffn_gain_sum, gain_start, gain_len, 0)
    scattered = (
        lax.psum_scatter(
            query_grad.astype(jnp.bfloat16), "dp", scatter_dimension=0, tiled=True
        ).astype(jnp.float32),
        lax.psum_scatter(
            key_grad.astype(jnp.bfloat16), "dp", scatter_dimension=0, tiled=True
        ).astype(jnp.float32),
        lax.psum_scatter(
            value_grad.astype(jnp.bfloat16), "dp", scatter_dimension=0, tiled=True
        ).astype(jnp.float32),
        lax.psum_scatter(
            gating_grad.astype(jnp.bfloat16), "dp", scatter_dimension=0, tiled=True
        ).astype(jnp.float32),
        lax.psum_scatter(
            alpha_grad.astype(jnp.bfloat16), "dp", scatter_dimension=0, tiled=True
        ).astype(jnp.float32),
        lax.psum_scatter(
            beta_grad.astype(jnp.bfloat16), "dp", scatter_dimension=0, tiled=True
        ).astype(jnp.float32),
        lax.psum_scatter(
            out_grad.astype(jnp.bfloat16), "dp", scatter_dimension=1, tiled=True
        ).astype(jnp.float32),
        lax.psum_scatter(
            gate_grad.astype(jnp.bfloat16), "dp", scatter_dimension=0, tiled=True
        ).astype(jnp.float32),
        lax.psum_scatter(
            up_grad.astype(jnp.bfloat16), "dp", scatter_dimension=0, tiled=True
        ).astype(jnp.float32),
        lax.psum_scatter(
            down_grad.astype(jnp.bfloat16), "dp", scatter_dimension=1, tiled=True
        ).astype(jnp.float32),
    )
    return (
        activations,
        loss,
        input_grad,
        attn_gain_out,
        scattered[0],
        scattered[1],
        scattered[2],
        scattered[3],
        scattered[4],
        scattered[5],
        q_conv_sum,
        k_conv_sum,
        v_conv_sum,
        decay_log_sum,
        decay_bias_sum,
        out_gain_sum,
        scattered[6],
        ffn_gain_out,
        scattered[7],
        scattered[8],
        scattered[9],
    )


def solution(mesh):
    placed = (
        P("dp", None, None),
        P("dp"),
        P("dp", None),
        P("dp", None, None),
        P("dp"),
        P("dp", "tensor"),
        P("dp", "tensor"),
        P("dp", "tensor"),
        P("dp", "tensor"),
        P("dp", "tensor"),
        P("dp", "tensor"),
        P(None, "tensor"),
        P(None, "tensor"),
        P(None, "tensor"),
        P("tensor"),
        P("tensor"),
        P(),
        P("tensor", "dp"),
        P("dp"),
        P("dp", "tensor"),
        P("dp", "tensor"),
        P("tensor", "dp"),
    )
    return jax.shard_map(
        body,
        mesh=mesh,
        in_specs=placed,
        out_specs=(
            P("dp", "tensor", None),
            P(),
            P("dp", "tensor", None),
            P("dp"),
            P("dp", "tensor"),
            P("dp", "tensor"),
            P("dp", "tensor"),
            P("dp", "tensor"),
            P("dp", "tensor"),
            P("dp", "tensor"),
            P(None, "tensor"),
            P(None, "tensor"),
            P(None, "tensor"),
            P("tensor"),
            P("tensor"),
            P(),
            P("tensor", "dp"),
            P("dp"),
            P("dp", "tensor"),
            P("dp", "tensor"),
            P("tensor", "dp"),
        ),
        check_vma=False,
    )
```

profile of v0, /device:TPU:0, one launch (start us, length us, event | category | flops | bytes accessed | tf_op | source)
XLA Modules:
  0.0 2651.2 jit_solution(14977413346396025215)
XLA Ops:
  11.5 22.4 all-gather
  37.3 26.5 %all_gather.58 = bf16[2048,4]{0,1:T(4,128)(2,1)S(1)} all-gather(bf16[256,4]{0,1:T(4,128)(2,1)S(1)} %copy-done.87), channel_id=1, replica_groups=mesh['dp'=8,'tensor'=4] {'dp'}, dimensions={0}, use_global_device_ids=true | all-gather | bytes 18432 | tf_op jit(solution)/shard_map/all_gather | solution.py:168
  68.8 26.2 all_gather.60
  135.6 51.2 %all-gather.16.cloned.1.call-done = bf16[2048,1024]{1,0:T(8,128)(2,1)} async-done(((bf16[256,1024]{1,0:T(8,128)(2,1)}), bf16[2048,1024]{1,0:T(8,128)(2,1)}) %all-gather.16.cloned.1.call-update) | async-done | bytes 4194320 | tf_op jit(solution)/shard_map/all_gather | solution.py:166
  198.9 17.7 reshape.1974
  224.0 451.7 %while.42 = (s32[]{:T(128)}, f32[1,4,128,256]{3,2,1,0:T(8,128)S(1)}, f32[16,1,4,64,256]{4,3,2,1,0:T(8,128)}, f32[16,1,4,128,256]{4,3,2,1,0:T(8,128)}, f32[16,1,4...) while((s32[]{:T(128)}, ...), condition=%wide.region_5.7_spmd.clone, body=%wide.region_3.6_spmd.clone.sunk | while | flops 479596864 | bytes 7988986 | solution.py:103
  225.0 19.7 custom-call.25
  253.2 19.7 custom-call.25
  281.5 19.7 custom-call.25
  309.7 19.7 custom-call.25
  337.9 19.7 custom-call.25
  366.2 19.7 custom-call.25
  394.4 19.7 custom-call.25
  422.6 19.7 custom-call.25
  450.9 19.7 custom-call.25
  479.1 19.7 custom-call.25
  507.3 19.7 custom-call.25
  535.5 19.7 custom-call.25
  563.8 19.7 custom-call.25
  592.0 19.7 custom-call.25
  620.2 19.7 custom-call.25
  648.5 19.7 custom-call.25
  689.9 12.8 multiply_convert_fusion.3
  713.1 17.9 all-gather.1
  731.0 51.4 %reduce-scatter.19.cloned.1.call-done = f32[1,256,2048]{2,1,0:T(8,128)} async-done(((f32[1,1024,2048]{2,1,0:T(8,128)}), f32[1,256,2048]{2,1,0:T(8,128)}) %reduce-scatter.19.cloned.1.call-update) | async-done | bytes 2097168 | tf_op jit(solution)/shard_map/reduce_scatter | solution.py:222
  788.9 88.6 %all-gather.26.cloned.1.call-done = bf16[2048,1408]{1,0:T(8,128)(2,1)} async-done(((bf16[256,1408]{1,0:T(8,128)(2,1)}), bf16[2048,1408]{1,0:T(8,128)(2,1)}) %all-gather.26.cloned.1.call-update) | async-done | bytes 5767184 | tf_op jit(solution)/shard_map/all_gather | solution.py:172
  877.6 34.9 %all-gather.24.cloned.1.call-done = bf16[1,1024,2048]{2,1,0:T(8,128)(2,1)} async-done(((bf16[1,256,2048]{2,1,0:T(8,128)(2,1)}), bf16[1,1024,2048]{2,1,0:T(8,128)(2,1)}) %all-gather.24.cloned.1.call-update) | async-done | bytes 4194320 | tf_op jit(solution)/shard_map/all_gather | solution.py:235
  912.5 12.1 fusion.214
  924.5 83.0 %all-gather.28.cloned.1.call-done = bf16[2048,1408]{1,0:T(8,128)(2,1)} async-done(((bf16[256,1408]{1,0:T(8,128)(2,1)}), bf16[2048,1408]{1,0:T(8,128)(2,1)}) %all-gather.28.cloned.1.call-update) | async-done | bytes 5767184 | tf_op jit(solution)/shard_map/all_gather | solution.py:173
  1007.6 13.1 multiply_convert_fusion.2
  1020.7 80.8 %all-gather.30.cloned.1.call-done = bf16[1408,2048]{1,0:T(8,128)(2,1)} async-done(((bf16[1408,256]{1,0:T(8,128)(2,1)}), bf16[1408,2048]{1,0:T(8,128)(2,1)}) %all-gather.30.cloned.1.call-update) | async-done | bytes 5767184 | tf_op jit(solution)/shard_map/all_gather | solution.py:174
  1101.5 11.5 convolution_bitcast_fusion.12
  1115.0 38.9 %psum.71 = f32[]{:T(128)} all-reduce(f32[]{:T(128)} %get-tuple-element.784), channel_id=1, replica_groups=mesh['dp'=8,'tensor'=4] {'dp','tensor'}, use_global_device_ids=true, to_apply=%region_13.15 | all-reduce | flops 1 | bytes 8 | tf_op jit(solution)/shard_map/psum | solution.py:247
  1154.6 29.2 %reduce-scatter.21.cloned.1.call-done = f32[1,256,2048]{2,1,0:T(8,128)} async-done(((f32[1,1024,2048]{2,1,0:T(8,128)}), f32[1,256,2048]{2,1,0:T(8,128)}) %reduce-scatter.21.cloned.1.call-update) | async-done | bytes 2097168 | tf_op jit(solution)/shard_map/reduce_scatter | solution.py:242
  1187.7 34.6 %all-gather.32.cloned.1.call-done = bf16[1,1024,2048]{2,1,0:T(8,128)(2,1)} async-done(((bf16[1,256,2048]{2,1,0:T(8,128)(2,1)}), bf16[1,1024,2048]{2,1,0:T(8,128)(2,1)}) %all-gather.32.cloned.1.call-update) | async-done | bytes 4194320 | tf_op jit(solution)/shard_map/all_gather | solution.py:282
  1222.3 14.3 multiply_convert_fusion
  1258.5 44.6 %reduce-scatter.23.cloned.1.call-done = bf16[1,256,2048]{2,1,0:T(8,128)(2,1)} async-done(((bf16[1,1024,2048]{2,1,0:T(8,128)(2,1)}), bf16[1,256,2048]{2,1,0:T(8,128)(2,1)}) %reduce-scatter.23.cloned.1.call-update) | async-done | bytes 1048592 | tf_op jit(solution)/shard_map/reduce_scatter | solution.py:293
  1346.2 11.0 convolution_convert_fusion.1
  1357.7 15.8 fusion.199
  1395.7 615.6 %while.43 = (s32[]{:T(128)}, f32[1,4,128,256]{2,3,1,0:T(8,128)S(1)}, f32[16,1,4,64,128]{4,3,0,2,1:T(8,128)}, f32[16,1,4,64,128]{4,3,0,2,1:T(8,128)}, f32[16,1,4,...) while((s32[]{:T(128)}, ...), condition=%wide.region_30.32_spmd.clone, body=%wide.region_18.31_spmd.clone.sunk | while | flops 1198483968 | bytes 23140360 | solution.py:103
  1401.0 19.7 custom-call.26
  1439.5 19.7 custom-call.26
  1478.0 19.7 custom-call.26
  1516.4 19.7 custom-call.26
  1554.9 19.7 custom-call.26
  1593.4 19.7 custom-call.26
  1631.9 19.7 custom-call.26
  1670.3 19.7 custom-call.26
  1708.7 19.7 custom-call.26
  1747.2 19.7 custom-call.26
  1785.7 19.7 custom-call.26
  1824.1 19.7 custom-call.26
  1862.6 19.7 custom-call.26
  1901.0 19.7 custom-call.26
  1939.4 19.7 custom-call.26
  1977.9 19.7 custom-call.26
  2145.3 16.4 fusion.220
  2198.6 37.5 %all-reduce.31 = (bf16[4,512]{1,0:T(4,128)(2,1)S(1)}, bf16[4,512]{1,0:T(4,128)(2,1)S(1)}, bf16[4,1024]{1,0:T(4,128)(2,1)S(1)}, bf16[4]{0:T(256)(128)(2,1)S(1)}, bf16[4]{0:T(256)(128)(2,1)S(1)}) all-reduce(bf16[4,512]{1,0:T(4,128)(2,1)S(1)} %add_convert_fusion.4, ...), channel_id=1, replica_groups=mesh['dp'=8,'tensor'=4] {'dp'}, use_global_device_ids=true, to_apply=%region_47.49 | all-reduce | flops 8200 | bytes 32800 | tf_op jit(solution)/shard_map/psum | solution.py:360
  2246.2 69.6 %reduce-scatter.27.cloned.1.call-done = bf16[256,512]{1,0:T(8,128)(2,1)} async-done(((bf16[2048,512]{1,0:T(8,128)(2,1)}), bf16[256,512]{1,0:T(8,128)(2,1)}) %reduce-scatter.27.cloned.1.call-update) | async-done | bytes 262160 | tf_op jit(solution)/shard_map/reduce_scatter | solution.py:372
  2317.6 44.4 %reduce-scatter.25.cloned.1.call-done = bf16[1,256,2048]{2,1,0:T(8,128)(2,1)} async-done(((bf16[1,1024,2048]{2,1,0:T(8,128)(2,1)}), bf16[1,256,2048]{2,1,0:T(8,128)(2,1)}) %reduce-scatter.25.cloned.1.call-update) | async-done | bytes 1048592 | tf_op jit(solution)/shard_map/reduce_scatter | solution.py:345
  2364.3 42.2 %all-reduce.30 = (f32[]{:T(128)}, f32[2048]{0:T(1024)S(1)}, f32[256]{0:T(256)}, f32[2048]{0:T(1024)S(1)}) all-reduce(f32[]{:T(128)} %get-tuple-element.698, f32[2048]{0:T(1024)S(1)} %get-tuple-element.699, f32[256]{0:T(256)S(1)} %copy-done.84, f32[2048]{0:T(1024)S(1)} %copy-done.58), channel_id=1, replica_groups=mesh['dp'=8,'tensor'=4] {'dp','tensor'}, use_global_device_ids=true, to_apply=%region_11.13 | all-reduce | flops 4353 | bytes 34824 | tf_op jit(solution)/shard_map/psum | solution.py:247
  2409.2 46.1 %reduce-scatter.35.cloned.1.call-done = bf16[1024,256]{1,0:T(8,128)(2,1)} async-done(((bf16[1024,2048]{1,0:T(8,128)(2,1)}), bf16[1024,256]{1,0:T(8,128)(2,1)}) %reduce-scatter.35.cloned.1.call-update) | async-done | bytes 524304 | tf_op jit(solution)/shard_map/reduce_scatter | solution.py:390
  2457.3 89.5 %reduce-scatter.31.cloned.1.call-done = bf16[256,1024]{1,0:T(8,128)(2,1)} async-done(((bf16[2048,1024]{1,0:T(8,128)(2,1)}), bf16[256,1024]{1,0:T(8,128)(2,1)}) %reduce-scatter.31.cloned.1.call-update) | async-done | bytes 524304 | tf_op jit(solution)/shard_map/reduce_scatter | solution.py:378
  2548.9 89.2 %reduce-scatter.33.cloned.1.call-done = bf16[256,1024]{1,0:T(8,128)(2,1)} async-done(((bf16[2048,1024]{1,0:T(8,128)(2,1)}), bf16[256,1024]{1,0:T(8,128)(2,1)}) %reduce-scatter.33.cloned.1.call-update) | async-done | bytes 524304 | tf_op jit(solution)/shard_map/reduce_scatter | solution.py:381
  (1494 shorter events, 823.7 us)
Async XLA Ops:
  7.2 29.9 %copy-start.80 = (f32[4,512]{1,0:T(4,128)S(1)}, f32[4,512]{1,0:T(4,128)}, u32[]{:S(2)}) copy-start(f32[4,512]{1,0:T(4,128)} %param.40) | copy-start | bytes 24580
  7.2 29.9 %copy-start.81 = (f32[4,512]{1,0:T(4,128)S(1)}, f32[4,512]{1,0:T(4,128)}, u32[]{:S(2)}) copy-start(f32[4,512]{1,0:T(4,128)} %param.39) | copy-start | bytes 24580
  7.2 30.0 %copy-start.77 = (f32[4,1024]{1,0:T(4,128)S(1)}, f32[4,1024]{1,0:T(4,128)}, u32[]{:S(2)}) copy-start(f32[4,1024]{1,0:T(4,128)} %param.41) | copy-start | bytes 49156
  7.2 30.0 %copy-start.87 = (bf16[256,4]{0,1:T(4,128)(2,1)S(1)}, bf16[256,4]{0,1:T(4,128)(2,1)}, u32[]{:S(2)}) copy-start(bf16[256,4]{0,1:T(4,128)(2,1)} %param.37) | copy-start | bytes 6148
  7.2 56.6 %copy-start.93 = (f32[4]{0:T(128)S(1)}, f32[4]{0:T(128)}, u32[]{:S(2)}) copy-start(f32[4]{0:T(128)} %param.42) | copy-start | bytes 52
  7.2 91.4 %all-gather.14.cloned.1.call-start = ((), (), s32[]{:S(2)}) async-start(), calls=%async_computation.14 | async-start | bytes 2359296 | tf_op jit(solution)/shard_map/all_gather | solution.py:165
  8.0 104.8 %all-gather.18.cloned.1.call-start = ((), (), s32[]{:S(2)}) async-start(), calls=%async_computation.16 | async-start | bytes 2359296 | tf_op jit(solution)/shard_map/all_gather | solution.py:164
  8.7 178.0 %all-gather.16.cloned.1.call-start = ((), (), s32[]{:S(2)}) async-start(), calls=%async_computation.15 | async-start | bytes 4718592 | tf_op jit(solution)/shard_map/all_gather | solution.py:166
  9.5 680.4 %all-gather.20.cloned.1.call-start = ((), (), s32[]{:S(2)}) async-start(), calls=%async_computation.17 | async-start | bytes 4718592 | tf_op jit(solution)/shard_map/all_gather | solution.py:167
  10.0 692.6 %all-gather.22.cloned.1.call-start = ((), (), s32[]{:S(2)}) async-start(), calls=%async_computation.18 | async-start | bytes 4718592 | tf_op jit(solution)/shard_map/all_gather | solution.py:170
  10.6 771.9 %reduce-scatter.19.cloned.1.call-start = ((), (), s32[]{:S(2)}) async-start(), calls=%async_computation.19 | async-start | bytes 10485760 | tf_op jit(solution)/shard_map/reduce_scatter | solution.py:222
  10.7 53.1 %copy-start.3 = (bf16[1,1024,2048]{2,1,0:T(8,128)(2,1)S(1)}, bf16[1,1024,2048]{2,1,0:T(8,128)(2,1)}, u32[]{:S(2)}) copy-start(bf16[1,1024,2048]{2,1,0:T(8,128)(2,1)} %param.28) | copy-start | bytes 12582916
  34.0 30.9 %copy-start.45 = (f32[8,1,256]{2,1,0:T(1,128)}, f32[8,1,256]{2,1,0:T(1,128)S(1)}, u32[]{:S(2)}) copy-start(f32[8,1,256]{2,1,0:T(1,128)S(1)} %convert_element_type.394) | copy-start | bytes 24580
  37.1 27.8 %copy-start.75 = (f32[1024]{0:T(1024)}, f32[1024]{0:T(1024)S(1)}, u32[]{:S(2)}) copy-start(f32[1024]{0:T(1024)S(1)} %add_rsqrt_fusion.2) | copy-start | bytes 12292
  37.1 66.7 %copy-start.67 = (f32[1,512]{1,0:T(1,128)}, f32[1,512]{1,0:T(1,128)S(1)}, u32[]{:S(2)}) copy-start(f32[1,512]{1,0:T(1,128)S(1)} %get-tuple-element.842) | copy-start | bytes 6148
  37.1 66.7 %copy-start.69 = (f32[1,512]{1,0:T(1,128)}, f32[1,512]{1,0:T(1,128)S(1)}, u32[]{:S(2)}) copy-start(f32[1,512]{1,0:T(1,128)S(1)} %get-tuple-element.843) | copy-start | bytes 6148
  37.1 66.7 %copy-start.71 = (f32[1,512]{1,0:T(1,128)}, f32[1,512]{1,0:T(1,128)S(1)}, u32[]{:S(2)}) copy-start(f32[1,512]{1,0:T(1,128)S(1)} %get-tuple-element.844) | copy-start | bytes 6148
  37.2 66.7 %copy-start.73 = (f32[1,512]{1,0:T(1,128)}, f32[1,512]{1,0:T(1,128)S(1)}, u32[]{:S(2)}) copy-start(f32[1,512]{1,0:T(1,128)S(1)} %get-tuple-element.845) | copy-start | bytes 6148
  37.2 80.7 %copy-start.59 = (f32[1,512]{1,0:T(1,128)}, f32[1,512]{1,0:T(1,128)S(1)}, u32[]{:S(2)}) copy-start(f32[1,512]{1,0:T(1,128)S(1)} %get-tuple-element.838) | copy-start | bytes 6148
  37.2 80.7 %copy-start.61 = (f32[1,512]{1,0:T(1,128)}, f32[1,512]{1,0:T(1,128)S(1)}, u32[]{:S(2)}) copy-start(f32[1,512]{1,0:T(1,128)S(1)} %get-tuple-element.839) | copy-start | bytes 6148
  37.2 80.7 %copy-start.63 = (f32[1,512]{1,0:T(1,128)}, f32[1,512]{1,0:T(1,128)S(1)}, u32[]{:S(2)}) copy-start(f32[1,512]{1,0:T(1,128)S(1)} %get-tuple-element.840) | copy-start | bytes 6148
  37.2 80.7 %copy-start.65 = (f32[1,512]{1,0:T(1,128)}, f32[1,512]{1,0:T(1,128)S(1)}, u32[]{:S(2)}) copy-start(f32[1,512]{1,0:T(1,128)S(1)} %get-tuple-element.841) | copy-start | bytes 6148
  37.3 157.0 %copy-start.50 = (f32[1,1024]{1,0:T(1,128)}, f32[1,1024]{1,0:T(1,128)S(1)}, u32[]{:S(2)}) copy-start(f32[1,1024]{1,0:T(1,128)S(1)} %get-tuple-element.834) | copy-start | bytes 12292
  37.3 157.0 %copy-start.52 = (f32[1,1024]{1,0:T(1,128)}, f32[1,1024]{1,0:T(1,128)S(1)}, u32[]{:S(2)}) copy-start(f32[1,1024]{1,0:T(1,128)S(1)} %get-tuple-element.835) | copy-start | bytes 12292
  37.3 157.0 %copy-start.54 = (f32[1,1024]{1,0:T(1,128)}, f32[1,1024]{1,0:T(1,128)S(1)}, u32[]{:S(2)}) copy-start(f32[1,1024]{1,0:T(1,128)S(1)} %get-tuple-element.836) | copy-start | bytes 12292
  37.3 157.0 %copy-start.56 = (f32[1,1024]{1,0:T(1,128)}, f32[1,1024]{1,0:T(1,128)S(1)}, u32[]{:S(2)}) copy-start(f32[1,1024]{1,0:T(1,128)S(1)} %get-tuple-element.837) | copy-start | bytes 12292
  66.9 31.6 %copy-start.78 = (f32[256]{0:T(256)S(1)}, f32[256]{0:T(256)}, u32[]{:S(2)}) copy-start(f32[256]{0:T(256)} %param.44) | copy-start | bytes 3076
  95.0 8.8 copy-start.35
  702.7 9.6 copy-start.95
  712.2 165.3 %all-gather.26.cloned.1.call-start = ((), (), s32[]{:S(2)}) async-start(), calls=%async_computation.21 | async-start | bytes 6488064 | tf_op jit(solution)/shard_map/all_gather | solution.py:172
  713.0 199.5 %all-gather.24.cloned.1.call-start = ((), (), s32[]{:S(2)}) async-start(), calls=%async_computation.20 | async-start | bytes 5242880 | tf_op jit(solution)/shard_map/all_gather | solution.py:235
  787.6 220.0 %all-gather.28.cloned.1.call-start = ((), (), s32[]{:S(2)}) async-start(), calls=%async_computation.22 | async-start | bytes 6488064 | tf_op jit(solution)/shard_map/all_gather | solution.py:173
  788.3 313.2 %all-gather.30.cloned.1.call-start = ((), (), s32[]{:S(2)}) async-start(), calls=%async_computation.23 | async-start | bytes 6488064 | tf_op jit(solution)/shard_map/all_gather | solution.py:174
  788.9 394.8 %reduce-scatter.21.cloned.1.call-start = ((), (), s32[]{:S(2)}) async-start(), calls=%async_computation.24 | async-start | bytes 10485760 | tf_op jit(solution)/shard_map/reduce_scatter | solution.py:242
  1112.9 109.3 %all-gather.32.cloned.1.call-start = ((), (), s32[]{:S(2)}) async-start(), calls=%async_computation.25 | async-start | bytes 5242880 | tf_op jit(solution)/shard_map/all_gather | solution.py:282
  1187.6 115.5 %reduce-scatter.23.cloned.1.call-start = ((), (), s32[]{:S(2)}) async-start(), calls=%async_computation.26 | async-start | bytes 5242880 | tf_op jit(solution)/shard_map/reduce_scatter | solution.py:293
  1236.6 10.8 copy-start.98
  1236.6 10.8 copy-start.100
  1258.4 99.3 %all-gather.34.cloned.1.call-start = ((), (), s32[]{:S(2)}) async-start(), calls=%async_computation.27 | async-start | bytes 5242880 | tf_op jit(solution)/shard_map/all_gather | solution.py:305
  1313.0 878.5 %reduce-scatter.41.cloned.1.call-start = ((), (), s32[]{:S(2)}) async-start(), calls=%async_computation.36 | async-start | bytes 6488064 | tf_op jit(solution)/shard_map/reduce_scatter | solution.py:399
  1323.8 870.0 %reduce-scatter.37.cloned.1.call-start = ((), (), s32[]{:S(2)}) async-start(), calls=%async_computation.34 | async-start | bytes 6488064 | tf_op jit(solution)/shard_map/reduce_scatter | solution.py:393
  1336.5 859.6 %reduce-scatter.39.cloned.1.call-start = ((), (), s32[]{:S(2)}) async-start(), calls=%async_computation.35 | async-start | bytes 6488064 | tf_op jit(solution)/shard_map/reduce_scatter | solution.py:396
  1357.3 881.6 %reduce-scatter.43.cloned.1.call-start = ((), (), s32[]{:S(2)}) async-start(), calls=%async_computation.37 | async-start | bytes 589824
  1379.3 7.6 copy-start.32
  1379.3 7.7 copy-start.1
  2046.5 193.9 %reduce-scatter.45.cloned.1.call-start = ((), (), s32[]{:S(2)}) async-start(), calls=%async_computation.38 | async-start | bytes 589824
  2050.5 193.8 %reduce-scatter.29.cloned.1.call-start = ((), (), s32[]{:S(2)}) async-start(), calls=%async_computation.30 | async-start | bytes 2359296 | tf_op jit(solution)/shard_map/reduce_scatter | solution.py:375
  2067.6 248.2 %reduce-scatter.27.cloned.1.call-start = ((), (), s32[]{:S(2)}) async-start(), calls=%async_computation.29 | async-start | bytes 2359296 | tf_op jit(solution)/shard_map/reduce_scatter | solution.py:372
  2095.1 10.7 copy-start.51
  2095.1 10.8 copy-start.53
  2095.1 10.8 copy-start.55
  2095.1 10.8 copy-start.57
  2112.5 249.5 %reduce-scatter.25.cloned.1.call-start = ((), (), s32[]{:S(2)}) async-start(), calls=%async_computation.28 | async-start | bytes 5242880 | tf_op jit(solution)/shard_map/reduce_scatter | solution.py:345
  2112.6 7.5 copy-start.19
  2112.6 7.5 copy-start.20
  2131.5 7.1 copy-start.96
  2161.8 293.4 %reduce-scatter.35.cloned.1.call-start = ((), (), s32[]{:S(2)}) async-start(), calls=%async_computation.33 | async-start | bytes 4718592 | tf_op jit(solution)/shard_map/reduce_scatter | solution.py:390
  2171.3 375.5 %reduce-scatter.31.cloned.1.call-start = ((), (), s32[]{:S(2)}) async-start(), calls=%async_computation.31 | async-start | bytes 4718592 | tf_op jit(solution)/shard_map/reduce_scatter | solution.py:378
  2180.7 457.4 %reduce-scatter.33.cloned.1.call-start = ((), (), s32[]{:S(2)}) async-start(), calls=%async_computation.32 | async-start | bytes 4718592 | tf_op jit(solution)/shard_map/reduce_scatter | solution.py:381
  2190.8 7.7 copy-start.94
  2193.8 170.5 %copy-start.58 = (f32[2048]{0:T(1024)S(1)}, f32[2048]{0:T(1024)}, u32[]{:S(2)}) copy-start(f32[2048]{0:T(1024)} %get-tuple-element.696) | copy-start | bytes 24580
  2193.8 170.5 %copy-start.84 = (f32[256]{0:T(256)S(1)}, f32[256]{0:T(256)}, u32[]{:S(2)}) copy-start(f32[256]{0:T(256)} %get-tuple-element.691) | copy-start | bytes 3076
  2242.0 398.3 %copy-start.21 = (f32[1,256,2048]{2,1,0:T(8,128)S(1)}, f32[1,256,2048]{2,1,0:T(8,128)}, u32[]{:S(2)}) copy-start(f32[1,256,2048]{2,1,0:T(8,128)} %get-tuple-element.783) | copy-start | bytes 6291460
  2362.0 278.2 %copy-start.26 = (bf16[1,256,2048]{2,1,0:T(8,128)(2,1)S(1)}, bf16[1,256,2048]{2,1,0:T(8,128)(2,1)}, u32[]{:S(2)}) copy-start(bf16[1,256,2048]{2,1,0:T(8,128)(2,1)} %reduce-scatter.25.cloned.1.call-done) | copy-start | bytes 3145732
  (62 other events, 250.0 us)
Sparse Core Ops, SparseCore 0:
  10.2 52.0 all-gather.13
  64.5 48.2 all-gather.17
  114.9 71.8 all-gather.15
  188.7 71.6 all-gather.19
  262.3 75.8 all-gather.21
  712.4 70.0 reduce-scatter.18
  784.9 92.6 all-gather.25
  879.8 32.6 all-gather.23
  914.9 92.6 all-gather.27
  1009.7 91.7 all-gather.29
  1113.1 70.6 reduce-scatter.20
  1187.7 34.4 all-gather.31
  1258.6 44.4 reduce-scatter.22
  1313.1 34.4 all-gather.33
  1351.6 110.3 reduce-scatter.40
  1466.0 109.7 reduce-scatter.36
  1579.7 109.8 reduce-scatter.38
  2046.7 62.2 reduce-scatter.42
  2112.9 60.9 reduce-scatter.44
  2177.7 66.6 reduce-scatter.28
  2248.9 66.8 reduce-scatter.26
  2318.5 43.4 reduce-scatter.24
  2365.6 89.5 reduce-scatter.34
  2459.1 87.6 reduce-scatter.30
  2550.4 87.6 reduce-scatter.32
where the time goes:
time: 2660 us; the launch traced here: 2650 us
  waiting for transfers between devices  845 us (32%)
  other arithmetic  837 us (31%)
  matrix products  533 us (20%)
  blocking collectives  212 us (8%)
  local copies, waits for them, and re-layouts  198 us (7%)
    another operation x112, other arithmetic, delta_block(): jax.scipy.linalg.solve_triangular(identity + key_mix, right_side, lower=T...  634 us
    dot_general x10, matrix products, back_product(): jnp.einsum('te,de->td', d_target, weight, preferred_element_type=jnp.floa...  99.8 us
    reduce_scatter x1, waiting for transfers between devices, body(): lax.psum_scatter(value_grad.astype(jnp.bfloat16), 'dp', scatter_dimension...  89.5 us
    reduce_scatter x1, waiting for transfers between devices, body(): lax.psum_scatter(gating_grad.astype(jnp.bfloat16), 'dp', scatter_dimensio...  89.2 us
    all_gather x1, waiting for transfers between devices, body(): lax.all_gather(ffn_gate, 'dp', axis=0, tiled=True)  88.6 us
    all_gather x1, waiting for transfers between devices, body(): lax.all_gather(ffn_up, 'dp', axis=0, tiled=True)  83 us
    psum x2, blocking collectives, body(): lax.psum((jnp.sum(error * error), jnp.sum(row_weight)), ('dp', 'tensor'))  81.2 us
    all_gather x1, waiting for transfers between devices, body(): lax.all_gather(ffn_down, 'dp', axis=1, tiled=True)  80.8 us
  transfers between devices with their start and end apart: 25, of which 16 were waited for; matrix products, arithmetic and copies ran while one was open for 56% of the time, Pallas kernels for 0%

commit v1 on v0

v1 whole, which is shorter than its diff:
```python
import functools
import jax
import jax.numpy as jnp
from jax import lax
from jax.experimental import pallas as pl
from jax.experimental.pallas import tpu as pltpu
from jax.sharding import PartitionSpec as P

BLOCK = 128
BF = jnp.bfloat16
F32 = jnp.float32


def mm(a, b, dims=((1,), (0,))):
    return lax.dot_general(a.astype(BF), b.astype(BF), (dims, ((), ())), preferred_element_type=F32)


def mm_nt(a, b):
    return mm(a, b, ((1,), (1,)))


def mm_tn(a, b):
    return mm(a, b, ((0,), (0,)))


def split(a):
    high = a.astype(BF)
    return high, (a - high.astype(F32)).astype(BF)


def mm3(a, b):
    ah, al = a
    bh, bl = b
    return mm(ah, bh) + (mm(ah, bl) + mm(al, bh))


def exact(a, b):
    return lax.dot_general(a, b, (((1,), (0,)), ((), ())), precision=lax.Precision.HIGHEST, preferred_element_type=F32)


def indices():
    rows = lax.broadcasted_iota(jnp.int32, (BLOCK, BLOCK), 0)
    cols = lax.broadcasted_iota(jnp.int32, (BLOCK, BLOCK), 1)
    return rows, cols


def unit_lower_inverse(strict, rows, cols):
    near = jnp.where((rows // 8) == (cols // 8), strict, 0.0)
    eye = (rows == cols).astype(F32)
    first = split(-near)
    second = mm3(first, first)
    second_s = split(second)
    fourth_s = split(mm3(second_s, second_s))
    total = eye - near
    total = total + mm3(split(total), second_s)
    total = total + mm3(split(total), fourth_s)
    size = 8
    while size < BLOCK:
        pick = ((rows // size) == (cols // size) + 1) & ((rows // size) % 2 == 1)
        lower = split(jnp.where(pick, strict, 0.0))
        total_s = split(total)
        total = total - mm3(total_s, split(mm3(lower, total_s)))
        size *= 2
    return total


def decay_terms(ab, hp, rows, cols):
    shifted = ab + hp[1:2, :]
    soft = jnp.maximum(shifted, 0.0) + jnp.log1p(jnp.exp(-jnp.abs(shifted)))
    decay = hp[0:1, :] * soft
    lower = (rows >= cols).astype(F32)
    cum = exact(lower, decay)
    return shifted, decay, cum


def conv_silu(ext_ref, taps, start, width):
    cols = slice(start, start + width)
    total = ext_ref[5 : 5 + BLOCK, cols] * taps[0:1, cols]
    for tap in range(1, 4):
        total = total + ext_ref[5 + tap : 5 + tap + BLOCK, cols] * taps[tap : tap + 1, cols]
    sig = jax.nn.sigmoid(total)
    return total, sig


def forward_kernel(
    heads, dk, dv, proj_ref, taps_ref, hp_ref, gain_ref,
    mixed_ref, o_ref, f_ref, t_ref, s_ref, state, ext,
):
    hk, hv = heads * dk, heads * dv
    wide = 2 * hk + hv

    @pl.when(pl.program_id(0) == 0)
    def _():
        state[...] = jnp.zeros_like(state)
        ext[0:8, :] = jnp.zeros((8, wide), F32)

    @pl.when(pl.program_id(0) > 0)
    def _():
        ext[0:8, :] = ext[BLOCK : BLOCK + 8, :]

    ext[8 : 8 + BLOCK, :] = proj_ref[:, 0:wide].astype(F32)
    rows, cols = indices()
    ab = proj_ref[:, wide + hv :].astype(F32)
    _, _, cum = decay_terms(ab, hp_ref[...], rows, cols)
    beta_all = jax.nn.sigmoid(ab)
    cum_t = cum.T
    within = rows >= cols
    strict = rows > cols
    taps = taps_ref[...]
    gain = gain_ref[...]
    s_ref[0] = state[...].astype(s_ref.dtype)
    for h in range(heads):
        raw, sig = conv_silu(ext, taps, h * dk, dk)
        act = raw * sig
        query = act * (lax.rsqrt(jnp.sum(act * act, -1, keepdims=True) + 1e-06) * dk ** (-0.5))
        raw, sig = conv_silu(ext, taps, hk + h * dk, dk)
        act = raw * sig
        key = act * lax.rsqrt(jnp.sum(act * act, -1, keepdims=True) + 1e-06)
        raw, sig = conv_silu(ext, taps, 2 * hk + h * dv, dv)
        value = raw * sig
        beta = beta_all[:, heads + h : heads + h + 1]
        c_col = cum[:, h : h + 1]
        c_row = cum_t[h : h + 1, :]
        c_last = cum[BLOCK - 1 : BLOCK, h : h + 1]
        fade = jnp.exp(jnp.where(within, c_col - c_row, 0.0))
        key_b = key.astype(BF)
        query_b = query.astype(BF)
        mix = jnp.where(strict, mm_nt(key_b, key_b) * fade * beta, 0.0)
        inverse = unit_lower_inverse(mix, rows, cols)
        inv_b = inverse.astype(BF)
        t_ref[:, h * BLOCK : (h + 1) * BLOCK] = inv_b
        grow = jnp.exp(c_col)
        w_rows = mm(inv_b, key * (beta * grow))
        u_rows = mm(inv_b, value * beta)
        memory = state[h * dk : (h + 1) * dk, :]
        mem_b = memory.astype(BF)
        fresh = u_rows - mm(w_rows, mem_b)
        fresh_b = fresh.astype(BF)
        f_ref[:, h * dv : (h + 1) * dv] = fresh_b
        scores = jnp.where(within, mm_nt(query_b, key_b) * fade, 0.0)
        out = mm(query_b, mem_b) * grow + mm(scores, fresh_b)
        state[h * dk : (h + 1) * dk, :] = jnp.exp(c_last) * memory + mm_tn(
            key * jnp.exp(c_last - c_col), fresh_b
        )
        o_ref[:, h * dv : (h + 1) * dv] = out.astype(o_ref.dtype)
        gate = proj_ref[:, wide + h * dv : wide + (h + 1) * dv].astype(F32)
        scale = lax.rsqrt(jnp.mean(out * out, -1, keepdims=True) + 1e-05)
        mixed_ref[:, h * dv : (h + 1) * dv] = (
            out * scale * gain * (gate * jax.nn.sigmoid(gate))
        ).astype(mixed_ref.dtype)


def delta_forward(proj, taps, hp, gain, heads, dk, dv, store=BF):
    rows = proj.shape[0]
    steps = rows // BLOCK
    wide = 2 * heads * dk + heads * dv
    width = proj.shape[1]
    hv = heads * dv

    def by_step(cols):
        return pl.BlockSpec((BLOCK, cols), lambda i: (i, 0))

    def fixed(shape):
        return pl.BlockSpec(shape, lambda i: (0, 0))

    return pl.pallas_call(
        functools.partial(forward_kernel, heads, dk, dv),
        grid=(steps,),
        in_specs=[by_step(width), fixed(taps.shape), fixed(hp.shape), fixed(gain.shape)],
        out_specs=[
            by_step(hv), by_step(hv), by_step(hv), by_step(heads * BLOCK),
            pl.BlockSpec((1, heads * dk, dv), lambda i: (i, 0, 0)),
        ],
        out_shape=[
            jax.ShapeDtypeStruct((rows, hv), BF),
            jax.ShapeDtypeStruct((rows, hv), store),
            jax.ShapeDtypeStruct((rows, hv), BF),
            jax.ShapeDtypeStruct((rows, heads * BLOCK), BF),
            jax.ShapeDtypeStruct((steps, heads * dk, dv), BF),
        ],
        scratch_shapes=[
            pltpu.VMEM((heads * dk, dv), F32),
            pltpu.VMEM((BLOCK + 8, wide), F32),
        ],
        compiler_params=pltpu.CompilerParams(dimension_semantics=("arbitrary",)),
        cost_estimate=pl.CostEstimate(flops=6 * rows * heads * 128 * 128 * 10, bytes_accessed=rows * 30000, transcendentals=0),
    )(proj, taps, hp, gain)


def unit_back(act, scale, grad):
    return scale * grad - act * (scale * scale * scale) * jnp.sum(grad * act, -1, keepdims=True)


def silu_back(raw, sig, grad):
    return grad * (sig * (1.0 + raw * (1.0 - sig)))


def backward_kernel(
    heads, dk, dv, proj_ref, halo_ref, taps_ref, hp_ref, gain_ref, o_ref, f_ref, t_ref, s_ref, dm_ref,
    dproj_ref, dtaps_ref, dhp_ref, dgain_ref, dstate, ext, dext,
):
    hk, hv = heads * dk, heads * dv
    wide = 2 * hk + hv
    step = pl.program_id(0)
    last = pl.num_programs(0) - 1

    @pl.when(step == 0)
    def _():
        dstate[...] = jnp.zeros_like(dstate)
        dext[BLOCK : BLOCK + 8, :] = jnp.zeros((8, wide), F32)
        dtaps_ref[...] = jnp.zeros_like(dtaps_ref)
        dhp_ref[...] = jnp.zeros_like(dhp_ref)
        dgain_ref[...] = jnp.zeros_like(dgain_ref)

    @pl.when(step > 0)
    def _():
        dext[BLOCK : BLOCK + 8, :] = dext[0:8, :]

    ext[0:8, :] = jnp.where(step == last, 0.0, halo_ref[:, 0:wide].astype(F32))
    ext[8 : 8 + BLOCK, :] = proj_ref[:, 0:wide].astype(F32)
    rows, cols = indices()
    ab = proj_ref[:, wide + hv :].astype(F32)
    hp = hp_ref[...]
    shifted, decay, cum = decay_terms(ab, hp, rows, cols)
    beta_all = jax.nn.sigmoid(ab)
    cum_t = cum.T
    within = rows >= cols
    strict = rows > cols
    taps = taps_ref[...]
    gain = gain_ref[...]
    lane = cols
    dbeta_all = jnp.zeros((BLOCK, BLOCK), F32)
    dcum_all = jnp.zeros((BLOCK, BLOCK), F32)
    dcum_rows = jnp.zeros((BLOCK, BLOCK), F32)
    dlast_all = jnp.zeros((1, BLOCK), F32)
    dgain = jnp.zeros((1, dv), F32)
    for h in range(heads):
        q_cols = slice(h * dk, (h + 1) * dk)
        k_cols = slice(hk + h * dk, hk + (h + 1) * dk)
        v_cols = slice(2 * hk + h * dv, 2 * hk + (h + 1) * dv)
        o_cols = slice(h * dv, (h + 1) * dv)
        gate = proj_ref[:, wide + h * dv : wide + (h + 1) * dv].astype(F32)
        out = o_ref[:, o_cols].astype(F32)
        d_mixed = dm_ref[:, o_cols].astype(F32)
        scale = lax.rsqrt(jnp.mean(out * out, -1, keepdims=True) + 1e-05)
        sig = jax.nn.sigmoid(gate)
        base = out * scale * d_mixed
        dgain = dgain + jnp.sum(base * (gate * sig), 0, keepdims=True)
        dproj_ref[:, wide + h * dv : wide + (h + 1) * dv] = silu_back(gate, sig, base * gain).astype(dproj_ref.dtype)
        d_normed = d_mixed * gain * (gate * sig)
        d_out = scale * d_normed - out * (scale * scale * scale) * jnp.mean(d_normed * out, -1, keepdims=True)
        d_out_b = d_out.astype(BF)
        q_raw, q_sig = conv_silu(ext, taps, h * dk, dk)
        q_act = q_raw * q_sig
        q_scale = lax.rsqrt(jnp.sum(q_act * q_act, -1, keepdims=True) + 1e-06)
        query = q_act * (q_scale * dk ** (-0.5))
        k_raw, k_sig = conv_silu(ext, taps, hk + h * dk, dk)
        k_act = k_raw * k_sig
        k_scale = lax.rsqrt(jnp.sum(k_act * k_act, -1, keepdims=True) + 1e-06)
        key = k_act * k_scale
        v_raw, v_sig = conv_silu(ext, taps, 2 * hk + h * dv, dv)
        value = v_raw * v_sig
        beta = beta_all[:, heads + h : heads + h + 1]
        c_col = cum[:, h : h + 1]
        c_row = cum_t[h : h + 1, :]
        c_last = cum[BLOCK - 1 : BLOCK, h : h + 1]
        fade = jnp.exp(jnp.where(within, c_col - c_row, 0.0))
        key_b = key.astype(BF)
        query_b = query.astype(BF)
        grow = jnp.exp(c_col)
        rest = jnp.exp(c_last - c_col)
        kk = jnp.where(strict, mm_nt(key_b, key_b) * fade, 0.0)
        scores = jnp.where(within, mm_nt(query_b, key_b) * fade, 0.0)
        inv_b = t_ref[:, h * BLOCK : (h + 1) * BLOCK]
        fresh_b = f_ref[:, o_cols]
        mem_b = s_ref[0, h * dk : (h + 1) * dk, :]
        d_mem = dstate[h * dk : (h + 1) * dk, :]
        d_mem_b = d_mem.astype(BF)
        d_fresh = mm_tn(scores, d_out_b) + mm(key * rest, d_mem_b)
        d_right = mm_tn(inv_b, d_fresh)
        d_right_b = d_right.astype(BF)
        d_scores = jnp.where(within, mm_nt(d_out_b, fresh_b), 0.0)
        d_mix = jnp.where(strict, -mm_nt(d_right_b, fresh_b), 0.0)
        x_rows = mm_nt(d_right_b, mem_b)
        y_rows = mm_nt(d_out_b, mem_b)
        z_rows = mm_nt(fresh_b, d_mem_b)
        decay_all = jnp.exp(c_last)
        dstate[h * dk : (h + 1) * dk, :] = (
            decay_all * d_mem
            + mm_tn(query * grow, d_out_b)
            - mm_tn(key * (beta * grow), d_right_b)
        )
        x_sum = jnp.sum(x_rows * key, -1, keepdims=True)
        y_sum = jnp.sum(y_rows * query, -1, keepdims=True)
        z_sum = jnp.sum(z_rows * key, -1, keepdims=True) * rest
        mix_part = d_mix * kk
        d_beta = (
            jnp.sum(d_right * value, -1, keepdims=True)
            - grow * x_sum
            + jnp.sum(mix_part, -1, keepdims=True)
        )
        pair = d_scores * scores + mix_part * beta
        d_cum = jnp.sum(pair, -1, keepdims=True) + grow * (y_sum - beta * x_sum) - z_sum
        d_last = jnp.sum(z_sum, 0, keepdims=True) + decay_all * jnp.sum(
            jnp.sum(d_mem * mem_b.astype(F32), -1, keepdims=True), 0, keepdims=True
        )
        dbeta_all = jnp.where(lane == heads + h, d_beta, dbeta_all)
        dcum_all = jnp.where(lane == h, d_cum, dcum_all)
        dcum_rows = jnp.where(rows == h, jnp.sum(pair, 0, keepdims=True), dcum_rows)
        dlast_all = jnp.where(lane[0:1, :] == h, d_last, dlast_all)
        g_scores = (d_scores * fade).astype(BF)
        g_mix = (d_mix * fade * beta).astype(BF)
        d_query = grow * y_rows + mm(g_scores, key_b)
        d_key = (
            rest * z_rows - (beta * grow) * x_rows
            + mm_tn(g_scores, query_b) + mm(g_mix, key_b) + mm_tn(g_mix, key_b)
        )
        d_value = d_right * beta
        dext[0:BLOCK, q_cols] = silu_back(q_raw, q_sig, unit_back(q_act, q_scale, d_query * dk ** (-0.5)))
        dext[0:BLOCK, k_cols] = silu_back(k_raw, k_sig, unit_back(k_act, k_scale, d_key))
        dext[0:BLOCK, v_cols] = silu_back(v_raw, v_sig, d_value)
    dgain_ref[...] += dgain
    d_cum = dcum_all - dcum_rows.T + jnp.where(rows == BLOCK - 1, dlast_all, 0.0)
    upper = (rows <= cols).astype(F32)
    d_decay = exact(upper, d_cum)
    d_alpha = d_decay * hp[0:1, :] * jax.nn.sigmoid(shifted)
    d_ab = d_alpha + dbeta_all * beta_all * (1.0 - beta_all)
    dproj_ref[:, wide + hv :] = d_ab.astype(dproj_ref.dtype)
    dhp_ref[0:1, :] += jnp.sum(d_decay * decay, 0, keepdims=True)
    dhp_ref[1:2, :] += jnp.sum(d_alpha, 0, keepdims=True)
    chunk = 256
    for start in range(0, wide, chunk):
        part = slice(start, start + chunk)
        d_conv = dext[0:BLOCK, part]
        total = dext[3 : 3 + BLOCK, part] * taps[0:1, part]
        dtaps_ref[0:1, part] += jnp.sum(d_conv * ext[5 : 5 + BLOCK, part], 0, keepdims=True)
        for tap in range(1, 4):
            total = total + dext[3 - tap : 3 - tap + BLOCK, part] * taps[tap : tap + 1, part]
            dtaps_ref[tap : tap + 1, part] += jnp.sum(d_conv * ext[5 + tap : 5 + tap + BLOCK, part], 0, keepdims=True)
        dproj_ref[:, part] = total.astype(dproj_ref.dtype)


def delta_backward(proj, taps, hp, gain, out, fresh, inverse, states, d_mixed, heads, dk, dv):
    rows, width = proj.shape
    steps = rows // BLOCK
    wide = 2 * heads * dk + heads * dv
    hv = heads * dv

    def by_step(cols):
        return pl.BlockSpec((BLOCK, cols), lambda i: (steps - 1 - i, 0))

    def fixed(shape):
        return pl.BlockSpec(shape, lambda i: (0, 0))

    per = BLOCK // 8
    return pl.pallas_call(
        functools.partial(backward_kernel, heads, dk, dv),
        grid=(steps,),
        in_specs=[
            by_step(width),
            pl.BlockSpec((8, width), lambda i: (jnp.maximum((steps - 1 - i) * per - 1, 0), 0)),
            fixed(taps.shape), fixed(hp.shape), fixed(gain.shape),
            by_step(hv), by_step(hv), by_step(heads * BLOCK),
            pl.BlockSpec((1, heads * dk, dv), lambda i: (steps - 1 - i, 0, 0)),
            by_step(hv),
        ],
        out_specs=[by_step(width), fixed((8, wide)), fixed((8, BLOCK)), fixed((1, dv))],
        out_shape=[
            jax.ShapeDtypeStruct((rows, width), BF),
            jax.ShapeDtypeStruct((8, wide), F32),
            jax.ShapeDtypeStruct((8, BLOCK), F32),
            jax.ShapeDtypeStruct((1, dv), F32),
        ],
        scratch_shapes=[
            pltpu.VMEM((heads * dk, dv), F32),
            pltpu.VMEM((BLOCK + 8, wide), F32),
            pltpu.VMEM((BLOCK + 8, wide), F32),
        ],
        compiler_params=pltpu.CompilerParams(dimension_semantics=("arbitrary",)),
        cost_estimate=pl.CostEstimate(flops=6 * rows * heads * 128 * 128 * 16, bytes_accessed=rows * 40000, transcendentals=0),
    )(proj, proj, taps, hp, gain, out, fresh, inverse, states, d_mixed)


def norm_back(values, rms_inv, gain, d_normed):
    scaled = d_normed * gain
    gain_grad = jnp.sum(d_normed * values * rms_inv, 0)
    d_values = rms_inv * scaled - values * rms_inv**3 * jnp.mean(scaled * values, -1, keepdims=True)
    return (d_values, gain_grad)


def weight_grad(source, d_target):
    return jnp.einsum("td,te->de", source, d_target, preferred_element_type=jnp.float32)


def back_product(d_target, weight):
    return jnp.einsum("te,de->td", d_target, weight, preferred_element_type=jnp.float32)


def body(
    inputs, lengths, loss_mask, teacher, attn_gain, q_weight, k_weight, v_weight, gating_weight,
    alpha_weight, beta_weight, q_conv, k_conv, v_conv, decay_log, decay_bias, out_gain, out_weight,
    ffn_gain, ffn_gate, ffn_up, ffn_down,
):
    seq_count, slot_n, width_n = inputs.shape
    tokens_n = seq_count * slot_n
    share_n = slot_n // lax.axis_size("tensor")
    share_start = lax.axis_index("tensor") * share_n
    share_rows = seq_count * share_n
    heads = decay_log.shape[0]
    hk = q_conv.shape[1]
    hv = v_conv.shape[1]
    dk, dv = hk // heads, hv // heads
    wide = 2 * hk + hv
    unit_n = ffn_gate.shape[1]
    local_d = q_weight.shape[0]

    positions = lax.broadcasted_iota(jnp.int32, (seq_count, slot_n), 1)
    valid = (positions < lengths[:, None]).astype(jnp.float32)
    tok_weight = valid * loss_mask.astype(jnp.float32)
    count_all = lax.psum(jnp.sum(tok_weight), "dp")

    spare = BLOCK - 2 * heads - 2
    packed = jnp.concatenate(
        [q_weight, k_weight, v_weight, gating_weight, alpha_weight, beta_weight,
         attn_gain[:, None], ffn_gain[:, None], jnp.zeros((local_d, spare), BF)], 1)
    proj_w = lax.all_gather(packed, "dp", axis=0, tiled=True)
    out_w = lax.all_gather(out_weight, "dp", axis=1, tiled=True)
    pair_w = lax.all_gather(jnp.concatenate([ffn_gate, ffn_up], 1), "dp", axis=0, tiled=True)
    down_w = lax.all_gather(ffn_down, "dp", axis=1, tiled=True)
    gain_at = wide + hv + 2 * heads
    gain_attn = proj_w[:, gain_at].astype(jnp.float32)
    gain_ffn = proj_w[:, gain_at + 1].astype(jnp.float32)

    flat_in = inputs.reshape(tokens_n, width_n).astype(jnp.float32)
    attn_rms = lax.rsqrt(jnp.mean(flat_in * flat_in, -1, keepdims=True) + 1e-06)
    normed = (flat_in * attn_rms * gain_attn).astype(BF)
    proj = jnp.dot(normed, proj_w, preferred_element_type=jnp.float32)
    taps = jnp.pad(jnp.concatenate([q_conv, k_conv, v_conv], 1), ((0, 4), (0, 0)))
    hp = jnp.zeros((8, BLOCK), jnp.float32).at[0, :heads].set(-jnp.exp(decay_log)).at[1, :heads].set(decay_bias)
    mixed_low, mix_out, fresh, inverse, states = delta_forward(proj, taps, hp, out_gain[None], heads, dk, dv)
    attn_part = jnp.dot(mixed_low, out_w, preferred_element_type=jnp.float32).astype(BF)

    def share_of(array):
        return lax.dynamic_slice_in_dim(array, share_start, share_n, 1)

    def scatter_rows(array):
        return lax.psum_scatter(array, "tensor", scatter_dimension=0, tiled=True).astype(jnp.float32)

    def gather_rows(array):
        return lax.all_gather(array, "tensor", axis=0, tiled=True)

    base_in = share_of(inputs).reshape(share_rows, width_n).astype(jnp.float32)
    base_rms = lax.rsqrt(jnp.mean(base_in * base_in, -1, keepdims=True) + 1e-06)
    row_weight = share_of(tok_weight).reshape(share_rows, 1)
    row_valid = share_of(valid).reshape(share_rows, 1)
    row_teacher = share_of(teacher).reshape(share_rows, width_n).astype(jnp.float32)
    resid = base_in + scatter_rows(attn_part)
    ffn_rms = lax.rsqrt(jnp.mean(resid * resid, -1, keepdims=True) + 1e-06)
    normed_ffn = gather_rows((resid * ffn_rms * gain_ffn).astype(BF))
    pre = jnp.dot(normed_ffn, pair_w, preferred_element_type=jnp.float32)
    gate_pre, up_pre = pre[:, :unit_n], pre[:, unit_n:]
    sig_gate = jax.nn.sigmoid(gate_pre)
    silu_gate = gate_pre * sig_gate
    hidden = (silu_gate * up_pre).astype(BF)
    ffn_part = jnp.dot(hidden, down_w, preferred_element_type=jnp.float32).astype(BF)
    output = resid + scatter_rows(ffn_part)
    error = (output - row_teacher) * row_weight
    coef = 0.5 * tokens_n * lax.axis_size("dp") / count_all
    d_output = 2.0 * coef * error * row_weight
    d_ffn = gather_rows(d_output.astype(BF))
    down_grad = weight_grad(hidden, d_ffn).astype(BF)
    d_hidden = back_product(d_ffn, down_w)
    d_gate = (d_hidden * up_pre * sig_gate * (1.0 + gate_pre * (1.0 - sig_gate))).astype(BF)
    d_up = (d_hidden * silu_gate).astype(BF)
    d_pair = jnp.concatenate([d_gate, d_up], 1)
    pair_grad = weight_grad(normed_ffn, d_pair).astype(BF)
    d_nffn = scatter_rows(back_product(d_pair, pair_w).astype(BF))
    d_resid_norm, ffn_gain_grad = norm_back(resid, ffn_rms, gain_ffn, d_nffn)
    d_resid = d_output + d_resid_norm
    d_attn = gather_rows(d_resid.astype(BF))
    out_grad = weight_grad(mixed_low, d_attn).astype(BF)
    d_mixed = back_product(d_attn, out_w).astype(BF)
    d_proj, tap_grad, hp_grad, out_gain_part = delta_backward(
        proj, taps, hp, out_gain[None], mix_out, fresh, inverse, states, d_mixed, heads, dk, dv)
    proj_grad = weight_grad(normed, d_proj).astype(BF)
    d_norm = scatter_rows(back_product(d_proj, proj_w).astype(BF))
    d_in_norm, attn_gain_grad = norm_back(base_in, base_rms, gain_attn, d_norm)
    input_grad = (d_resid + d_in_norm).reshape(seq_count, share_n, width_n)
    activations = (output * row_valid).astype(BF).reshape(seq_count, share_n, width_n)

    down_sum = lax.psum_scatter(down_grad, "dp", scatter_dimension=1, tiled=True).astype(jnp.float32)
    pair_sum = lax.psum_scatter(pair_grad, "dp", scatter_dimension=0, tiled=True).astype(jnp.float32)
    out_sum = lax.psum_scatter(out_grad, "dp", scatter_dimension=1, tiled=True).astype(jnp.float32)
    proj_sum = lax.psum_scatter(proj_grad, "dp", scatter_dimension=0, tiled=True).astype(jnp.float32)

    error_all, gains_all, out_gain_sum = lax.psum(
        (jnp.sum(error * error), jnp.concatenate([attn_gain_grad, ffn_gain_grad]), out_gain_part[0]), ("dp", "tensor"))
    loss = error_all / count_all
    gain_len = width_n // lax.axis_size("dp")
    gain_start = lax.axis_index("dp") * gain_len
    attn_gain_out = lax.dynamic_slice_in_dim(gains_all, gain_start, gain_len, 0)
    ffn_gain_out = lax.dynamic_slice_in_dim(gains_all, width_n + gain_start, gain_len, 0)
    small = jnp.concatenate([tap_grad[:4], jnp.pad(hp_grad[:4], ((0, 0), (0, 0)))], 1)
    small = lax.psum(small, "dp")
    return (
        activations, loss, input_grad, attn_gain_out,
        proj_sum[:, :hk], proj_sum[:, hk : 2 * hk], proj_sum[:, 2 * hk : wide], proj_sum[:, wide : wide + hv],
        proj_sum[:, wide + hv : wide + hv + heads], proj_sum[:, wide + hv + heads : wide + hv + 2 * heads],
        small[:, :hk], small[:, hk : 2 * hk], small[:, 2 * hk : wide],
        small[0, wide : wide + heads], small[1, wide : wide + heads], out_gain_sum,
        out_sum, ffn_gain_out, pair_sum[:, :unit_n], pair_sum[:, unit_n:], down_sum,
    )


def solution(mesh):
    both = P("dp", "tensor")
    rows = P("dp", "tensor", None)
    flip = P("tensor", "dp")
    taps = P(None, "tensor")
    return jax.shard_map(
        body,
        mesh=mesh,
        in_specs=(
            P("dp", None, None), P("dp"), P("dp", None), P("dp", None, None), P("dp"),
            both, both, both, both, both, both, taps, taps, taps,
            P("tensor"), P("tensor"), P(), flip, P("dp"), both, both, flip,
        ),
        out_specs=(
            rows, P(), rows, P("dp"), both, both, both, both, both, both,
            taps, taps, taps, P("tensor"), P("tensor"), P(), flip, P("dp"), both, both, flip,
        ),
        check_vma=False,
    )
```

time: 2660 us -> 1560 us (0.59)
  other arithmetic: 837 us -> 36.7 us
  matrix products: 533 us -> 177 us
  waiting for transfers between devices: 845 us -> 1050 us
  local copies, waits for them, and re-layouts: 198 us -> 30.3 us
  Pallas kernels: 0 us -> 141 us
  blocking collectives: 212 us -> 96.2 us
    another operation x192 -> x1, other arithmetic: 651 us -> 0.01 us  [the longest x112 634 us: delta_block(): jax.scipy.linalg.solve_triangular(identity + key_mix, right_side, lower=T...]
    dot_general x362 -> x4, matrix products: 330 us -> 60.2 us  [the longest x1 23 us: body(): proj = jnp.dot(normed, proj_w, preferred_element_type=jnp.float32)]
    pallas_call x0 -> x2, Pallas kernels: none -> 141 us  [the longest x1 84.2 us: delta_forward(): pl.pallas_call(functools.partial(forward_kernel, heads, dk, dv), grid=(st...]
    all_gather x11 -> x7, waiting for transfers between devices: 374 us -> 507 us  [the longest x1 181 us: body(): proj_w = lax.all_gather(packed, 'dp', axis=0, tiled=True)]
    all_gather x4 -> x0, blocking collectives: 93.1 us -> none  [the longest x1 26.5 us: body(): lax.all_gather(alpha_weight, 'dp', axis=0, tiled=True)]
    reduce_scatter x12 -> x8, waiting for transfers between devices: 466 us -> 543 us  [the longest x1 211 us: body(): lax.psum_scatter(proj_grad, 'dp', scatter_dimension=0, tiled=True)]
    reduce_sum x59 -> x1, other arithmetic: 50.4 us -> 0.61 us  [body(): count_all = lax.psum(jnp.sum(tok_weight), 'dp')]
    squeeze x64 -> x1, local copies, waits for them, and re-layouts: 44.6 us -> 0.52 us  [body(): small[1, wide:wide + heads]]
  transfers between devices with their start and end apart: 25 -> 15, of which waited for: 16 -> 12; matrix products, arithmetic and copies ran while one was open for 56% -> 10% of each run, Pallas kernels for 0% -> 9%
where the time goes in v1:
time: 1560 us; the launch traced here: 1550 us
  waiting for transfers between devices  1050 us (67%)
  matrix products  177 us (11%)
  Pallas kernels  141 us (9%)
  blocking collectives  96.2 us (6%)
  other arithmetic  36.7 us (2%)
  local copies, waits for them, and re-layouts  30.3 us (2%)
  between operations  18.4 us (1%)
    reduce_scatter x1, waiting for transfers between devices, body(): lax.psum_scatter(proj_grad, 'dp', scatter_dimension=0, tiled=True)  211 us
    reduce_scatter x1, waiting for transfers between devices, body(): lax.psum_scatter(pair_grad, 'dp', scatter_dimension=0, tiled=True)  194 us
    all_gather x1, waiting for transfers between devices, body(): proj_w = lax.all_gather(packed, 'dp', axis=0, tiled=True)  181 us
    all_gather x1, waiting for transfers between devices, body(): lax.all_gather(jnp.concatenate([ffn_gate, ffn_up], 1), 'dp', axis=0, tile...  161 us
    reduce_scatter x4, waiting for transfers between devices, scatter_rows(): lax.psum_scatter(array, 'tensor', scatter_dimension=0, tiled=True)  106 us
    all_gather x3, waiting for transfers between devices, gather_rows(): return lax.all_gather(array, 'tensor', axis=0, tiled=True)  93.2 us
    pallas_call x1, Pallas kernels, delta_forward(): pl.pallas_call(functools.partial(forward_kernel, heads, dk, dv), grid=(st...  84.2 us
    all_gather x1, waiting for transfers between devices, body(): down_w = lax.all_gather(ffn_down, 'dp', axis=1, tiled=True)  72.4 us
  transfers between devices with their start and end apart: 15, of which 12 were waited for; matrix products, arithmetic and copies ran while one was open for 10% of the time, Pallas kernels for 9%

profile of v1, /device:TPU:0, one launch (start us, length us, event | category | flops | bytes accessed | tf_op | source)
XLA Modules:
  0.0 1554.3 jit_solution(10325495610084256969)
XLA Ops:
  7.3 0.8 broadcast_in_dim.12
  8.0 0.8 broadcast_in_dim.13
  8.8 0.8 copy.47
  9.6 0.8 copy.48
  10.5 3.8 concatenate.22
  14.3 0.7 all-gather.10.cloned.1.call-update
  15.3 3.1 fusion
  18.5 0.6 select_maximum_fusion.taps_ref
  19.1 180.9 %all-gather.8.cloned.1.call-done = bf16[2048,3200]{1,0:T(8,128)(2,1)} async-done(((bf16[256,3200]{1,0:T(8,128)(2,1)}), bf16[2048,3200]{1,0:T(8,128)(2,1)}) %all-gather.8.cloned.1.call-update) | async-done | bytes 13107216 | tf_op jit(solution)/shard_map/all_gather | solution.py:426
  200.0 1.9 convert_reduce_fusion
  201.9 23.0 %fusion.23.proj_ref.halo_ref = f32[1024,3200]{1,0:T(8,128)} fusion(bf16[2048,3200]{1,0:T(8,128)(2,1)} %all-gather.8.cloned.1.call-done, bf16[1,1024,2048]{2,1,0:T(8,128)(2,1)} %param.26, f32[2048]{0:T(1024)S(1)} %get-tuple-element.106, f32[1024]{0:T(1024)S(1)} %add_rsqrt_fusion), kind=kOutput, calls=%fused_computation.54 | convolution fusion | flops 13430161408 | bytes 30420992 | tf_op jit(solution)/shard_map/dot_general | solution.py:437
  224.9 84.2 %shard_map.373 = (bf16[1024,1024]{1,0:T(8,128)(2,1)}, bf16[1024,1024]{1,0:T(8,128)(2,1)}, bf16[1024,1024]{1,0:T(8,128)(2,1)}, bf16[1024,512]{1,0:T(8,128)(2,1)}, bf16[8,512,256]{2,1,0:T(8,128)(2,1)}) custom-call(f32[1024,3200]{1,0:T(8,128)} %fusion.23.proj_ref.halo_ref, f32[8,2048]{1,0:T(8,128)} %select_maximum_fusion.taps_ref, f32[8,128]{1,0:T(8,128)} %copy-done.14, ...), custom_call_target="tpu_custom_call" | custom-call | flops 4026531840 | bytes 30720000 | tf_op jit(solution)/shard_map/pallas_call | solution.py:166
  309.1 9.3 convolution_convert_fusion.7
  318.4 1.0 copy-done.8
  319.7 1.2 pad_maximum_fusion.3
  321.0 40.3 %reduce-scatter.9.cloned.1.call-done = bf16[256,2048]{1,0:T(8,128)(2,1)} async-done(((bf16[1024,2048]{1,0:T(8,128)(2,1)}), bf16[256,2048]{1,0:T(8,128)(2,1)}) %reduce-scatter.9.cloned.1.call-update) | async-done | bytes 1048592 | tf_op jit(solution)/shard_map/reduce_scatter | solution.py:447
  361.2 2.0 multiply_reduce_fusion.1
  363.2 2.9 multiply_convert_fusion.4
  366.8 161.0 %all-gather.14.cloned.1.call-done = bf16[2048,2816]{1,0:T(8,128)(2,1)} async-done(((bf16[256,2816]{1,0:T(8,128)(2,1)}), bf16[2048,2816]{1,0:T(8,128)(2,1)}) %all-gather.14.cloned.1.call-update) | async-done | bytes 11534352 | tf_op jit(solution)/shard_map/all_gather | solution.py:428
  527.8 34.8 %all-gather.12.cloned.1.call-done = bf16[1024,2048]{1,0:T(8,128)(2,1)} async-done(((bf16[256,2048]{1,0:T(8,128)(2,1)}), bf16[1024,2048]{1,0:T(8,128)(2,1)}) %all-gather.12.cloned.1.call-update) | async-done | bytes 4194320 | tf_op jit(solution)/shard_map/all_gather | solution.py:450
  562.5 17.2 %fusion.37 = f32[1024,2816]{1,0:T(8,128)S(1)} fusion(bf16[1024,2048]{1,0:T(8,128)(2,1)} %all-gather.12.cloned.1.call-done, bf16[2048,2816]{1,0:T(8,128)(2,1)} %all-gather.14.cloned.1.call-done), kind=kOutput, calls=%fused_computation.88 | convolution fusion | flops 11811160064 | bytes 27262976 | tf_op jit(solution)/shard_map/dot_general | solution.py:460
  579.7 4.3 copy-done.1
  584.0 1.8 multiply_convert_fusion.2
  585.8 72.4 %all-gather.16.cloned.1.call-done = bf16[1408,2048]{1,0:T(8,128)(2,1)} async-done(((bf16[1408,256]{1,0:T(8,128)(2,1)}), bf16[1408,2048]{1,0:T(8,128)(2,1)}) %all-gather.16.cloned.1.call-update) | async-done | bytes 5767184 | tf_op jit(solution)/shard_map/all_gather | solution.py:429
  658.3 10.8 convolution_convert_fusion.5
  670.1 0.6 fusion.30
  670.7 19.2 %psum.36 = f32[]{:T(128)} all-reduce(f32[]{:T(128)} %get-tuple-element.118), channel_id=1, replica_groups=mesh['dp'=8,'tensor'=4] {'dp'}, use_global_device_ids=true, to_apply=%region_7.8 | all-reduce | flops 1 | bytes 8 | tf_op jit(solution)/shard_map/psum | solution.py:420
  690.6 21.4 %reduce-scatter.11.cloned.1.call-done = bf16[256,2048]{1,0:T(8,128)(2,1)} async-done(((bf16[1024,2048]{1,0:T(8,128)(2,1)}), bf16[256,2048]{1,0:T(8,128)(2,1)}) %reduce-scatter.11.cloned.1.call-update) | async-done | bytes 1048592 | tf_op jit(solution)/shard_map/reduce_scatter | solution.py:447
  712.0 3.6 fusion.21
  715.6 34.6 %all-gather.18.cloned.1.call-done = bf16[1024,2048]{1,0:T(8,128)(2,1)} async-done(((bf16[256,2048]{1,0:T(8,128)(2,1)}), bf16[1024,2048]{1,0:T(8,128)(2,1)}) %all-gather.18.cloned.1.call-update) | async-done | bytes 4194320 | tf_op jit(solution)/shard_map/all_gather | solution.py:450
  750.2 14.1 multiply_convert_fusion.1
  764.3 1.6 copy-done.25
  765.9 0.9 copy-done.27
  766.8 16.3 %convolution_convert_fusion.4 = bf16[1024,2048]{1,0:T(8,128)(2,1)} fusion(bf16[2048,2816]{1,0:T(8,128)(2,1)} %all-gather.14.cloned.1.call-done, bf16[1024,1408]{1,0:T(8,128)(2,1)S(1)} %get-tuple-element.121, bf16[1024,1408]{1,0:T(8,128)(2,1)S(1)} %get-tuple-element.120), kind=kOutput, calls=%fused_computation.20 | convolution fusion | flops 11824791552 | bytes 21495808 | tf_op jit(solution)/shard_map/te,de->td/dot_general | solution.py:396
  783.2 44.6 %reduce-scatter.13.cloned.1.call-done = bf16[256,2048]{1,0:T(8,128)(2,1)} async-done(((bf16[1024,2048]{1,0:T(8,128)(2,1)}), bf16[256,2048]{1,0:T(8,128)(2,1)}) %reduce-scatter.13.cloned.1.call-update) | async-done | bytes 1048592 | tf_op jit(solution)/shard_map/reduce_scatter | solution.py:447
  827.8 4.3 fusion.14
  832.1 4.9 fusion.28
  837.1 10.5 convolution_convert_fusion.2
  847.9 23.8 %all-gather.20.cloned.1.call-done = bf16[1024,2048]{1,0:T(8,128)(2,1)} async-done(((bf16[256,2048]{1,0:T(8,128)(2,1)}), bf16[1024,2048]{1,0:T(8,128)(2,1)}) %all-gather.20.cloned.1.call-update) | async-done | bytes 4194320 | tf_op jit(solution)/shard_map/all_gather | solution.py:450
  871.7 9.3 convolution_convert_fusion.8.dm_ref
  881.0 57.2 %shard_map.374 = (bf16[1024,3200]{1,0:T(8,128)(2,1)}, f32[8,2048]{1,0:T(8,128)}, f32[8,128]{1,0:T(8,128)}, f32[1,256]{1,0:T(1,128)}) custom-call(f32[1024,3200]{1,0:T(8,128)} %fusion.23.proj_ref.halo_ref, f32[1024,3200]{1,0:T(8,128)} %fusion.23.proj_ref.halo_ref, f32[8,2048]{1,0:T(8,128)} %select_maximum_fusion.taps_ref, f32[8,128]{1,0:T(8,128)} %copy-done.14, ...), custom_call_target="tpu_custom_call" | custom-call | flops 6442450944 | bytes 40960000 | tf_op jit(solution)/shard_map/pallas_call | solution.py:356
  938.1 20.0 %convolution_convert_fusion.3 = bf16[1024,2048]{1,0:T(8,128)(2,1)} fusion(bf16[1024,3200]{1,0:T(8,128)(2,1)} %get-tuple-element.59, bf16[2048,3200]{1,0:T(8,128)(2,1)} %all-gather.8.cloned.1.call-done), kind=kOutput, calls=%fused_computation.19 | convolution fusion | flops 13423869952 | bytes 23855104 | tf_op jit(solution)/shard_map/te,de->td/dot_general | solution.py:396
  958.6 1.2 copy-done.24
  959.8 8.4 convolution_convert_fusion.6
  968.2 1.7 copy-done.26
  970.0 17.5 %convolution_convert_fusion.1 = bf16[2048,2816]{1,0:T(8,128)(2,1)} fusion(bf16[1024,2048]{1,0:T(8,128)(2,1)} %all-gather.12.cloned.1.call-done, bf16[1024,1408]{1,0:T(8,128)(2,1)} %copy-done.27, bf16[1024,1408]{1,0:T(8,128)(2,1)S(1)} %copy-done.26), kind=kOutput, calls=%fused_computation.1 | convolution fusion | flops 11828461568 | bytes 21495808 | tf_op jit(solution)/shard_map/td,te->de/dot_general | solution.py:392
  988.2 21.2 %convolution_convert_fusion = bf16[2048,3200]{1,0:T(8,128)(2,1)} fusion(bf16[1024,3200]{1,0:T(8,128)(2,1)} %get-tuple-element.59, bf16[1,1024,2048]{2,1,0:T(8,128)(2,1)} %param.26, f32[2048]{0:T(1024)S(1)} %copy-done.11, f32[1024]{0:T(1024)S(1)} %copy-done.19), kind=kOutput, calls=%fused_computation | convolution fusion | flops 13436715008 | bytes 23867392 | tf_op jit(solution)/shard_map/td,te->de/dot_general | solution.py:392
  1009.4 2.3 convert_element_type.165
  1011.8 37.6 %psum.38 = f32[4,2176]{1,0:T(4,128)S(1)} all-reduce(f32[4,2176]{1,0:T(4,128)S(1)} %pad_maximum_fusion.4), channel_id=1, replica_groups=mesh['dp'=8,'tensor'=4] {'dp'}, use_global_device_ids=true, to_apply=%region_17.18 | all-reduce | flops 8704 | bytes 69632 | tf_op jit(solution)/shard_map/psum | solution.py:504
  1049.5 0.6 slice.123
  1051.2 2.2 fusion.19
  1053.4 39.4 %all-reduce.2 = (f32[]{:T(128)}, f32[4096]{0:T(1024)S(1)}, f32[256]{0:T(256)}) all-reduce(f32[]{:T(128)} %get-tuple-element.111, f32[4096]{0:T(1024)S(1)} %pad_maximum_fusion.5, f32[256]{0:T(256)S(1)} %bitcast.80), channel_id=1, replica_groups=mesh['dp'=8,'tensor'=4] {'dp','tensor'}, use_global_device_ids=true, to_apply=%region_5.6 | all-reduce | flops 4353 | bytes 34824 | tf_op jit(solution)/shard_map/psum | solution.py:496
  1094.2 32.1 %reduce-scatter.19.cloned.1.call-done = bf16[1024,256]{1,0:T(8,128)(2,1)} async-done(((bf16[1024,2048]{1,0:T(8,128)(2,1)}), bf16[1024,256]{1,0:T(8,128)(2,1)}) %reduce-scatter.19.cloned.1.call-update) | async-done | bytes 524304 | tf_op jit(solution)/shard_map/reduce_scatter | solution.py:493
  1126.2 2.1 convert_element_type.161
  1128.3 0.6 fusion.36
  1128.9 193.6 %reduce-scatter.21.cloned.1.call-done = bf16[256,2816]{1,0:T(8,128)(2,1)} async-done(((bf16[2048,2816]{1,0:T(8,128)(2,1)}), bf16[256,2816]{1,0:T(8,128)(2,1)}) %reduce-scatter.21.cloned.1.call-update) | async-done | bytes 1441808 | tf_op jit(solution)/shard_map/reduce_scatter | solution.py:492
  1322.5 3.1 fusion.34
  1325.6 3.1 fusion.9
  1328.8 211.4 %reduce-scatter.17.cloned.1.call-done = bf16[256,3200]{1,0:T(8,128)(2,1)} async-done(((bf16[2048,3200]{1,0:T(8,128)(2,1)}), bf16[256,3200]{1,0:T(8,128)(2,1)}) %reduce-scatter.17.cloned.1.call-update) | async-done | bytes 1638416 | tf_op jit(solution)/shard_map/reduce_scatter | solution.py:494
  1540.2 1.1 fusion.31
  1541.2 0.7 copy.51
  1541.9 0.7 copy.52
  1542.6 2.8 fusion.32
  1545.3 1.1 fusion.33
  (100 shorter events, 4.5 us)
Async XLA Ops:
  7.2 7.9 copy-start.23
  7.2 7.9 copy-start.22
  7.2 192.8 %all-gather.8.cloned.1.call-start = ((), (), s32[]{:S(2)}) async-start(), calls=%async_computation.8 | async-start | bytes 14745600 | tf_op jit(solution)/shard_map/all_gather | solution.py:426
  10.4 8.0 copy-start.13
  10.4 8.0 copy-start.15
  10.5 8.0 copy-start.16
  14.3 294.8 %all-gather.10.cloned.1.call-start = ((), (), s32[]{:S(2)}) async-start(), calls=%async_computation.9 | async-start | bytes 4718592 | tf_op jit(solution)/shard_map/all_gather | solution.py:427
  15.0 346.2 %reduce-scatter.9.cloned.1.call-start = ((), (), s32[]{:S(2)}) async-start(), calls=%async_computation.10 | async-start | bytes 5242880 | tf_op jit(solution)/shard_map/reduce_scatter | solution.py:447
  15.3 209.6 %copy-start.14 = (f32[8,128]{1,0:T(8,128)}, f32[8,128]{1,0:T(8,128)S(1)}, u32[]{:S(2)}) copy-start(f32[8,128]{1,0:T(8,128)S(1)} %scatter.9.hp_ref) | copy-start | bytes 12292
  18.5 206.4 %copy-start.18 = (f32[1024]{0:T(1024)}, f32[1024]{0:T(1024)S(1)}, u32[]{:S(2)}) copy-start(f32[1024]{0:T(1024)S(1)} %add_rsqrt_fusion) | copy-start | bytes 12292
  201.9 23.0 %copy-start.10 = (f32[2048]{0:T(1024)}, f32[2048]{0:T(1024)S(1)}, u32[]{:S(2)}) copy-start(f32[2048]{0:T(1024)S(1)} %get-tuple-element.106) | copy-start | bytes 24580
  318.3 1.1 copy-start.8
  318.4 1.3 copy-start.9
  318.4 209.4 %all-gather.14.cloned.1.call-start = ((), (), s32[]{:S(2)}) async-start(), calls=%async_computation.12 | async-start | bytes 12976128 | tf_op jit(solution)/shard_map/all_gather | solution.py:428
  320.9 241.6 %all-gather.12.cloned.1.call-start = ((), (), s32[]{:S(2)}) async-start(), calls=%async_computation.11 | async-start | bytes 5242880 | tf_op jit(solution)/shard_map/all_gather | solution.py:450
  366.1 292.1 %all-gather.16.cloned.1.call-start = ((), (), s32[]{:S(2)}) async-start(), calls=%async_computation.13 | async-start | bytes 6488064 | tf_op jit(solution)/shard_map/all_gather | solution.py:429
  366.7 345.2 %reduce-scatter.11.cloned.1.call-start = ((), (), s32[]{:S(2)}) async-start(), calls=%async_computation.14 | async-start | bytes 5242880 | tf_op jit(solution)/shard_map/reduce_scatter | solution.py:447
  579.7 4.3 copy-start.1
  585.8 72.5 %copy-start.7 = (bf16[1024,1408]{1,0:T(8,128)(2,1)}, bf16[1024,1408]{1,0:T(8,128)(2,1)S(1)}, u32[]{:S(2)}) copy-start(bf16[1024,1408]{1,0:T(8,128)(2,1)S(1)} %multiply_convert_fusion.2) | copy-start | bytes 8650756
  669.1 1.0 copy-start.17
  669.1 42.9 %copy-start = (bf16[256,2048]{1,0:T(8,128)(2,1)S(1)}, bf16[256,2048]{1,0:T(8,128)(2,1)}, u32[]{:S(2)}) copy-start(bf16[256,2048]{1,0:T(8,128)(2,1)} %reduce-scatter.9.cloned.1.call-done) | copy-start | bytes 3145732
  669.1 81.1 %all-gather.18.cloned.1.call-start = ((), (), s32[]{:S(2)}) async-start(), calls=%async_computation.15 | async-start | bytes 5242880 | tf_op jit(solution)/shard_map/all_gather | solution.py:450
  715.6 112.2 %reduce-scatter.13.cloned.1.call-start = ((), (), s32[]{:S(2)}) async-start(), calls=%async_computation.16 | async-start | bytes 5242880 | tf_op jit(solution)/shard_map/reduce_scatter | solution.py:447
  764.3 1.6 copy-start.25
  764.3 2.5 copy-start.27
  783.1 44.7 %copy-start.2 = (bf16[256,2048]{1,0:T(8,128)(2,1)S(1)}, bf16[256,2048]{1,0:T(8,128)(2,1)}, u32[]{:S(2)}) copy-start(bf16[256,2048]{1,0:T(8,128)(2,1)} %reduce-scatter.11.cloned.1.call-done) | copy-start | bytes 3145732
  783.1 88.5 %all-gather.20.cloned.1.call-start = ((), (), s32[]{:S(2)}) async-start(), calls=%async_computation.17 | async-start | bytes 5242880 | tf_op jit(solution)/shard_map/all_gather | solution.py:450
  827.8 4.3 copy-start.6
  837.0 172.4 %reduce-scatter.23.cloned.1.call-start = ((), (), s32[]{:S(2)}) async-start(), calls=%async_computation.22 | async-start | bytes 6488064 | tf_op jit(solution)/shard_map/reduce_scatter | solution.py:491
  847.6 203.6 %reduce-scatter.15.cloned.1.call-start = ((), (), s32[]{:S(2)}) async-start(), calls=%async_computation.18 | async-start | bytes 5242880 | tf_op jit(solution)/shard_map/reduce_scatter | solution.py:447
  958.1 1.6 copy-start.24
  958.1 168.1 %reduce-scatter.19.cloned.1.call-start = ((), (), s32[]{:S(2)}) async-start(), calls=%async_computation.20 | async-start | bytes 4718592 | tf_op jit(solution)/shard_map/reduce_scatter | solution.py:493
  968.2 1.8 copy-start.26
  968.2 354.4 %reduce-scatter.21.cloned.1.call-start = ((), (), s32[]{:S(2)}) async-start(), calls=%async_computation.21 | async-start | bytes 12976128 | tf_op jit(solution)/shard_map/reduce_scatter | solution.py:492
  987.5 0.7 copy-start.11
  987.5 0.7 copy-start.19
  987.5 552.7 %reduce-scatter.17.cloned.1.call-start = ((), (), s32[]{:S(2)}) async-start(), calls=%async_computation.19 | async-start | bytes 14745600 | tf_op jit(solution)/shard_map/reduce_scatter | solution.py:494
  1009.4 2.4 copy-start.12
  1009.4 2.4 copy-start.21
  1009.4 44.0 %copy-start.20 = (f32[1,256]{1,0:T(1,128)S(1)}, f32[1,256]{1,0:T(1,128)}, u32[]{:S(2)}) copy-start(f32[1,256]{1,0:T(1,128)} %get-tuple-element.62) | copy-start | bytes 3076
  1053.4 272.3 %copy-start.3 = (f32[256,2048]{1,0:T(8,128)S(1)}, f32[256,2048]{1,0:T(8,128)}, u32[]{:S(2)}) copy-start(f32[256,2048]{1,0:T(8,128)} %get-tuple-element.117) | copy-start | bytes 6291460
  1053.4 272.3 %copy-start.5 = (bf16[256,2048]{1,0:T(8,128)(2,1)S(1)}, bf16[256,2048]{1,0:T(8,128)(2,1)}, u32[]{:S(2)}) copy-start(bf16[256,2048]{1,0:T(8,128)(2,1)} %reduce-scatter.15.cloned.1.call-done) | copy-start | bytes 3145732
  1540.2 5.2 copy-start.4
Sparse Core Ops, SparseCore 0:
  14.4 185.5 all-gather.7
  202.0 73.3 all-gather.9
  318.5 42.7 reduce-scatter.8
  364.1 163.6 all-gather.13
  529.8 32.6 all-gather.11
  564.6 93.5 all-gather.15
  669.2 42.6 reduce-scatter.10
  715.7 34.4 all-gather.17
  783.2 44.5 reduce-scatter.12
  837.1 34.4 all-gather.19
  875.8 110.3 reduce-scatter.22
  988.7 44.2 reduce-scatter.14
  1036.7 89.4 reduce-scatter.18
  1130.1 192.4 reduce-scatter.20
  1326.5 213.6 reduce-scatter.16

commit v2 on v1

--- a/solution.py
+++ b/solution.py
@@ -83,11 +83,13 @@
 
 
 def forward_kernel(
-    heads, dk, dv, proj_ref, taps_ref, hp_ref, gain_ref,
-    mixed_ref, o_ref, f_ref, t_ref, s_ref, state, ext,
+    heads, dk, dv, n, grid_n, ring_spec, proj_ref, taps_ref, hp_ref, gain_ref, shard_a, shard_b,
+    mixed_ref, o_ref, f_ref, t_ref, s_ref, whole_a, whole_b, state, ext, *sems,
 ):
     hk, hv = heads * dk, heads * dv
     wide = 2 * hk + hv
+    ring = RingGather(n, *ring_spec, (shard_a, shard_b), (whole_a, whole_b), sems)
+    hosted(ring, n, grid_n)
 
     @pl.when(pl.program_id(0) == 0)
     def _():
@@ -149,8 +151,13 @@
             out * scale * gain * (gate * jax.nn.sigmoid(gate))
         ).astype(mixed_ref.dtype)
 
-
-def delta_forward(proj, taps, hp, gain, heads, dk, dv, store=BF):
+    @pl.when(pl.program_id(0) == grid_n - 1)
+    def _():
+        ring.finish()
+
+
+def delta_forward(proj, taps, hp, gain, shards, kinds, n, heads, dk, dv, store=BF):
+    ring_spec = ([s.shape for s in shards], kinds, (2, 2))
     rows = proj.shape[0]
     steps = rows // BLOCK
     wide = 2 * heads * dk + heads * dv
@@ -164,12 +171,13 @@
         return pl.BlockSpec(shape, lambda i: (0, 0))
 
     return pl.pallas_call(
-        functools.partial(forward_kernel, heads, dk, dv),
+        functools.partial(forward_kernel, heads, dk, dv, n, steps, ring_spec),
         grid=(steps,),
-        in_specs=[by_step(width), fixed(taps.shape), fixed(hp.shape), fixed(gain.shape)],
+        in_specs=[by_step(width), fixed(taps.shape), fixed(hp.shape), fixed(gain.shape), ANYWHERE, ANYWHERE],
         out_specs=[
             by_step(hv), by_step(hv), by_step(hv), by_step(heads * BLOCK),
             pl.BlockSpec((1, heads * dk, dv), lambda i: (i, 0, 0)),
+            ANYWHERE, ANYWHERE,
         ],
         out_shape=[
             jax.ShapeDtypeStruct((rows, hv), BF),
@@ -177,14 +185,16 @@
             jax.ShapeDtypeStruct((rows, hv), BF),
             jax.ShapeDtypeStruct((rows, heads * BLOCK), BF),
             jax.ShapeDtypeStruct((steps, heads * dk, dv), BF),
+            *[jax.ShapeDtypeStruct(whole_shape(n, s.shape, k), BF) for s, k in zip(shards, kinds)],
         ],
         scratch_shapes=[
             pltpu.VMEM((heads * dk, dv), F32),
             pltpu.VMEM((BLOCK + 8, wide), F32),
+            *RingGather.scratch(n, ring_spec[0], ring_spec[2]),
         ],
-        compiler_params=pltpu.CompilerParams(dimension_semantics=("arbitrary",)),
+        compiler_params=comm_params(2),
         cost_estimate=pl.CostEstimate(flops=6 * rows * heads * 128 * 128 * 10, bytes_accessed=rows * 30000, transcendentals=0),
-    )(proj, taps, hp, gain)
+    )(proj, taps, hp, gain, *shards)
 
 
 def unit_back(act, scale, grad):
@@ -196,11 +206,13 @@
 
 
 def backward_kernel(
-    heads, dk, dv, proj_ref, halo_ref, taps_ref, hp_ref, gain_ref, o_ref, f_ref, t_ref, s_ref, dm_ref,
-    dproj_ref, dtaps_ref, dhp_ref, dgain_ref, dstate, ext, dext,
+    heads, dk, dv, n, grid_n, ring_spec, proj_ref, halo_ref, taps_ref, hp_ref, gain_ref, o_ref, f_ref, t_ref, s_ref,
+    dm_ref, grad_a, grad_b, dproj_ref, dtaps_ref, dhp_ref, dgain_ref, sum_a, sum_b, dstate, ext, dext, *scratch,
 ):
     hk, hv = heads * dk, heads * dv
     wide = 2 * hk + hv
+    ring = RingScatter(n, *ring_spec, (grad_a, grad_b), (sum_a, sum_b), scratch)
+    hosted(ring, n, grid_n)
     step = pl.program_id(0)
     last = pl.num_programs(0) - 1
 
@@ -339,8 +351,15 @@
             dtaps_ref[tap : tap + 1, part] += jnp.sum(d_conv * ext[5 + tap : 5 + tap + BLOCK, part], 0, keepdims=True)
         dproj_ref[:, part] = total.astype(dproj_ref.dtype)
 
-
-def delta_backward(proj, taps, hp, gain, out, fresh, inverse, states, d_mixed, heads, dk, dv):
+    @pl.when(step == grid_n - 1)
+    def _():
+        ring.finish()
+
+
+def delta_backward(
+    proj, taps, hp, gain, out, fresh, inverse, states, d_mixed, grads, shapes, kinds, n, heads, dk, dv,
+):
+    ring_spec = (shapes, kinds, (2, 2))
     rows, width = proj.shape
     steps = rows // BLOCK
     wide = 2 * heads * dk + heads * dv
@@ -354,7 +373,7 @@
 
     per = BLOCK // 8
     return pl.pallas_call(
-        functools.partial(backward_kernel, heads, dk, dv),
+        functools.partial(backward_kernel, heads, dk, dv, n, steps, ring_spec),
         grid=(steps,),
         in_specs=[
             by_step(width),
@@ -362,34 +381,725 @@
             fixed(taps.shape), fixed(hp.shape), fixed(gain.shape),
             by_step(hv), by_step(hv), by_step(heads * BLOCK),
             pl.BlockSpec((1, heads * dk, dv), lambda i: (steps - 1 - i, 0, 0)),
-            by_step(hv),
+            by_step(hv), ANYWHERE, ANYWHERE,
         ],
-        out_specs=[by_step(width), fixed((8, wide)), fixed((8, BLOCK)), fixed((1, dv))],
+        out_specs=[
+            by_step(width), fixed((8, wide)), fixed((8, BLOCK)), fixed((1, dv)), *[fixed(s) for s in shapes],
+        ],
         out_shape=[
             jax.ShapeDtypeStruct((rows, width), BF),
             jax.ShapeDtypeStruct((8, wide), F32),
             jax.ShapeDtypeStruct((8, BLOCK), F32),
             jax.ShapeDtypeStruct((1, dv), F32),
+            *[jax.ShapeDtypeStruct(s, F32) for s in shapes],
         ],
         scratch_shapes=[
             pltpu.VMEM((heads * dk, dv), F32),
             pltpu.VMEM((BLOCK + 8, wide), F32),
             pltpu.VMEM((BLOCK + 8, wide), F32),
+            *RingScatter.scratch(n, shapes, ring_spec[2]),
         ],
-        compiler_params=pltpu.CompilerParams(dimension_semantics=("arbitrary",)),
+        compiler_params=comm_params(9),
         cost_estimate=pl.CostEstimate(flops=6 * rows * heads * 128 * 128 * 16, bytes_accessed=rows * 40000, transcendentals=0),
-    )(proj, proj, taps, hp, gain, out, fresh, inverse, states, d_mixed)
+    )(proj, proj, taps, hp, gain, out, fresh, inverse, states, d_mixed, *grads)
+
+
+MESH = pl.DeviceIdType.MESH
+
+
+def ring_place(index, n):
+    half = index // 2
+    return half + (index % 2) * (n - 1 - 2 * half)
+
+
+def ring_index(place, n):
+    far = place // (n // 2)
+    return (1 - far) * 2 * place + far * (2 * (n - 1 - place) + 1)
+
+
+class Ring:
+    def __init__(self, n, shapes, kinds, parts):
+        self.n, self.shapes, self.kinds, self.parts = n, shapes, kinds, parts
+        self.place = ring_place(lax.axis_index("dp"), n)
+        self.next = ring_index((self.place + 1) % n, n)
+        self.prev = ring_index((self.place + n - 1) % n, n)
+
+    def greet(self, barrier):
+        for device in (self.next, self.prev):
+            pl.semaphore_signal(barrier, inc=1, device_id={"dp": device}, device_id_type=MESH)
+        return 2
+
+    def pieces(self):
+        stream = 0
+        for i, (rows, _) in enumerate(self.shapes):
+            size = rows // (2 * self.parts[i])
+            for part in range(self.parts[i]):
+                for way in range(2):
+                    yield stream, i, way, (way * self.parts[i] + part) * size, size
+                    stream += 1
+
+    def window(self, ref, i, block, offset, size):
+        rows, cols = self.shapes[i]
+        if self.kinds[i] == "rows":
+            return ref.at[pl.ds(pl.multiple_of(block * rows + offset, 16), size), :]
+        if self.kinds[i] == "cols":
+            return ref.at[pl.ds(offset, size), pl.ds(pl.multiple_of(block * cols, 128), cols)]
+        return ref.at[block, pl.ds(offset, size), :]
+
+    def send(self, source, target, send_sem, recv_sem, way):
+        return pltpu.make_async_remote_copy(
+            src_ref=source, dst_ref=target, send_sem=send_sem, recv_sem=recv_sem,
+            device_id={"dp": self.next if way == 0 else self.prev}, device_id_type=MESH)
+
+
+def ring_streams(parts):
+    return 2 * sum(parts)
+
+
+class RingGather(Ring):
+    def __init__(self, n, shapes, kinds, parts, shards, wholes, sems, starts=None):
+        super().__init__(n, shapes, kinds, parts)
+        self.shards, self.wholes = shards, wholes
+        self.send_sem, self.recv_sem, self.own_sem = sems
+
+    @staticmethod
+    def scratch(n, shapes, parts):
+        count = ring_streams(parts)
+        dma = pltpu.SemaphoreType.DMA
+        return [dma((n - 1, count)), dma((n - 1, count)), dma((len(shapes),))]
+
+    def copies(self, step):
+        made = []
+        for stream, i, way, offset, size in self.pieces():
+            ahead = self.n - step if way == 0 else step
+            block = ring_index((self.place + ahead) % self.n, self.n)
+            there = self.window(self.wholes[i], i, block, offset, size)
+            first = isinstance(step, int) and step == 0
+            here = self.shards[i].at[pl.ds(offset, size), :] if first else there
+            made.append(self.send(here, there, self.send_sem.at[step, stream], self.recv_sem.at[step, stream], way))
+        return made
+
+    def own(self):
+        me = lax.axis_index("dp")
+        return [
+            pltpu.make_async_copy(shard, self.window(whole, i, me, 0, self.shapes[i][0]), self.own_sem.at[i])
+            for i, (shard, whole) in enumerate(zip(self.shards, self.wholes))
+        ]
+
+    def start(self):
+        for copy in self.copies(0) + self.own():
+            copy.start()
+
+    def step(self, step):
+        for old, new in zip(self.copies(step - 1), self.copies(step)):
+            old.wait_recv()
+            new.start()
+
+    def finish(self):
+        for copy in self.copies(self.n - 2):
+            copy.wait_recv()
+
+        def done(step, carry):
+            for copy in self.copies(step):
+                copy.wait_send()
+            return carry
+
+        lax.fori_loop(0, self.n - 1, done, 0)
+        for copy in self.own():
+            copy.wait()
+
+
+class RingScatter(Ring):
+    def __init__(self, n, shapes, kinds, parts, grads, results, scratch):
+        super().__init__(n, shapes, kinds, parts)
+        count = len(shapes)
+        self.grads, self.results = grads, results
+        self.slots, self.mine = scratch[:count], scratch[count : 2 * count]
+        self.send_sem, self.recv_sem, self.load_sem = scratch[2 * count :]
+
+    @staticmethod
+    def scratch(n, shapes, parts):
+        count = ring_streams(parts)
+        dma = pltpu.SemaphoreType.DMA
+        return (
+            [pltpu.VMEM((n - 1, rows, cols), BF) for rows, cols in shapes]
+            + [pltpu.VMEM((2, rows, cols), BF) for rows, cols in shapes]
+            + [dma((n - 1, count)), dma((n - 1, count)), dma((2, count))]
+        )
+
+    def grad(self, step, i, way, offset, size):
+        ahead = 2 * self.n - 1 - step if way == 0 else 1 + step
+        block = ring_index((self.place + ahead) % self.n, self.n)
+        return self.window(self.grads[i], i, block, offset, size)
+
+    def copy(self, step, piece):
+        stream, i, way, offset, size = piece
+        rows = pl.ds(offset, size)
+        if isinstance(step, int) and step == 0:
+            here = self.grad(0, i, way, offset, size)
+        else:
+            here = self.slots[i].at[step - 1, rows, :]
+        return self.send(
+            here, self.slots[i].at[step, rows, :], self.send_sem.at[step, stream], self.recv_sem.at[step, stream], way)
+
+    def arrival(self, step, piece):
+        stream, i, way, offset, size = piece
+        slot = self.slots[i].at[step, pl.ds(offset, size), :]
+        return self.send(slot, slot, self.send_sem.at[step, stream], self.recv_sem.at[step, stream], way)
+
+    def load(self, step, piece):
+        stream, i, way, offset, size = piece
+        half = step % 2
+        return pltpu.make_async_copy(
+            self.grad(step, i, way, offset, size), self.mine[i].at[half, pl.ds(offset, size), :],
+            self.load_sem.at[half, stream])
+
+    def start(self):
+        for piece in self.pieces():
+            self.copy(0, piece).start()
+        for piece in self.pieces():
+            self.load(1, piece).start()
+
+    def add(self, step, piece, store):
+        _, i, _, offset, size = piece
+        high = 16
+
+        def rows(k, carry):
+            at = pl.ds(pl.multiple_of(offset + k * high, high), high)
+            total = self.slots[i][step - 1, at, :].astype(F32) + self.mine[i][step % 2, at, :].astype(F32)
+            store(i, at, total)
+            return carry
+
+        lax.fori_loop(0, size // high, rows, 0)
+
+    def step(self, step):
+        for piece in self.pieces():
+            self.load(step + 1, piece).start()
+        for piece in self.pieces():
+            self.arrival(step - 1, piece).wait_recv()
+            self.load(step, piece).wait()
+
+            def store(i, at, total):
+                self.slots[i][step - 1, at, :] = total.astype(BF)
+
+            self.add(step, piece, store)
+            self.copy(step, piece).start()
+
+    def finish(self):
+        last = self.n - 1
+        for piece in self.pieces():
+            self.arrival(last - 1, piece).wait_recv()
+            self.load(last, piece).wait()
+
+            def store(i, at, total):
+                self.results[i][at, :] = total
+
+            self.add(last, piece, store)
+
+        def done(step, carry):
+            for piece in self.pieces():
+                self.arrival(step, piece).wait_send()
+            return carry
+
+        lax.fori_loop(0, self.n - 1, done, 0)
+
+
+class Quad:
+    def __init__(self):
+        me = lax.axis_index("tensor")
+        self.me = me
+        self.near = me + 1 - 2 * (me % 2)
+        self.far = (me + 2) % 4
+        self.cross = (self.near + 2) % 4
+
+    def greet(self, barrier):
+        for device in (self.near, self.far):
+            pl.semaphore_signal(barrier, inc=1, device_id={"tensor": device}, device_id_type=MESH)
+        return 2
+
+    @staticmethod
+    def send(source, target, send_sem, recv_sem, device):
+        return pltpu.make_async_remote_copy(
+            src_ref=source, dst_ref=target, send_sem=send_sem, recv_sem=recv_sem,
+            device_id={"tensor": device}, device_id_type=MESH)
+
+
+class QuadGather(Quad):
+    def __init__(self, rows, parts, shard, whole, sems):
+        super().__init__()
+        self.rows, self.parts, self.shard, self.whole = rows, parts, shard, whole
+        self.send_sem, self.recv_sem, self.own_sem = sems
+
+    @staticmethod
+    def scratch(parts):
+        dma = pltpu.SemaphoreType.DMA
+        return [dma((3, parts)), dma((3, parts)), dma((1,))]
+
+    def at(self, block, part):
+        size = self.rows // self.parts
+        return self.whole.at[pl.ds(pl.multiple_of(block * self.rows + part * size, 16), size), :]
+
+    def copy(self, kind, part):
+        size = self.rows // self.parts
+        here = self.shard.at[pl.ds(part * size, size), :]
+        sems = (self.send_sem.at[kind, part], self.recv_sem.at[kind, part])
+        if kind == 0:
+            return self.send(here, self.at(self.me, part), *sems, self.far)
+        if kind == 1:
+            return self.send(here, self.at(self.me, part), *sems, self.near)
+        return self.send(self.at(self.far, part), self.at(self.far, part), *sems, self.near)
+
+    def own(self):
+        return pltpu.make_async_copy(
+            self.shard, self.whole.at[pl.ds(pl.multiple_of(self.me * self.rows, 16), self.rows), :], self.own_sem.at[0])
+
+    def start(self):
+        for part in range(self.parts):
+            self.copy(0, part).start()
+        for part in range(self.parts):
+            self.copy(1, part).start()
+        self.own().start()
+
+    def step(self, part):
+        self.copy(0, part).wait_recv()
+        self.copy(2, part).start()
+
+    def finish(self):
+        for part in range(self.parts):
+            self.copy(1, part).wait_recv()
+            self.copy(2, part).wait_recv()
+            for kind in range(3):
+                self.copy(kind, part).wait_send()
+        self.own().wait()
+
+
+class QuadScatter(Quad):
+    def __init__(self, rows, parts, partial, result, scratch):
+        super().__init__()
+        self.rows, self.parts, self.partial, self.result = rows, parts, partial, result
+        self.pair, self.mine, self.other, self.send_sem, self.recv_sem, self.load_sem = scratch
+
+    @staticmethod
+    def scratch(rows, cols, parts):
+        dma = pltpu.SemaphoreType.DMA
+        return [
+            pltpu.VMEM((2, rows, cols), BF), pltpu.VMEM((2, rows, cols), BF), pltpu.VMEM((rows, cols), BF),
+            dma((3, parts)), dma((3, parts)), dma((2, parts)),
+        ]
+
+    def part_rows(self, part):
+        size = self.rows // self.parts
+        return pl.ds(part * size, size)
+
+    def at(self, block, part):
+        size = self.rows // self.parts
+        return self.partial.at[pl.ds(pl.multiple_of(block * self.rows + part * size, 16), size), :]
+
+    def copy(self, kind, part):
+        rows = self.part_rows(part)
+        sems = (self.send_sem.at[kind, part], self.recv_sem.at[kind, part])
+        if kind == 0:
+            return self.send(self.at(self.cross, part), self.pair.at[0, rows, :], *sems, self.near)
+        if kind == 1:
+            return self.send(self.at(self.near, part), self.pair.at[1, rows, :], *sems, self.near)
+        return self.send(self.pair.at[0, rows, :], self.other.at[rows, :], *sems, self.far)
+
+    def load(self, kind, part):
+        block = self.far if kind == 0 else self.me
+        return pltpu.make_async_copy(
+            self.at(block, part), self.mine.at[kind, self.part_rows(part), :], self.load_sem.at[kind, part])
+
+    def start(self):
+        for kind in range(2):
+            for part in range(self.parts):
+                self.copy(kind, part).start()
+                self.load(kind, part).start()
+
+    def over(self, part, work):
+        size = self.rows // self.parts
+        high = 16
+
+        def rows(k, carry):
+            work(pl.ds(pl.multiple_of(part * size + k * high, high), high))
+            return carry
+
+        lax.fori_loop(0, size // high, rows, 0)
+
+    def step(self, part):
+        self.copy(0, part).wait_recv()
+        self.load(0, part).wait()
+
+        def work(at):
+            total = self.pair[0, at, :].astype(F32) + self.mine[0, at, :].astype(F32)
+            self.pair[0, at, :] = total.astype(BF)
+
+        self.over(part, work)
+        self.copy(2, part).start()
+
+    def finish(self):
+        for part in range(self.parts):
+            self.copy(1, part).wait_recv()
+            self.load(1, part).wait()
+            self.copy(2, part).wait_recv()
+
+            def work(at):
+                near = self.pair[1, at, :].astype(F32) + self.mine[1, at, :].astype(F32)
+                self.result[at, :] = near + self.other[at, :].astype(F32)
+
+            self.over(part, work)
+        for part in range(self.parts):
+            for kind in range(3):
+                self.copy(kind, part).wait_send()
+
+
+def meet(*groups):
+    barrier = pltpu.get_barrier_semaphore()
+    pl.semaphore_wait(barrier, sum(group.greet(barrier) for group in groups))
+
+
+def run_between(ring, first, stop):
+    def body(step, carry):
+        ring.step(step)
+        return carry
+
+    lax.fori_loop(first, stop, body, 0)
+
+
+def interleave(ring, quad, n):
+    total = n - 2
+    for part in range(quad.parts):
+        quad.step(part)
+        run_between(ring, 1 + total * part // quad.parts, 1 + total * (part + 1) // quad.parts)
+
+
+def hosted(ring, n, grid_n):
+    here = pl.program_id(0)
+
+    @pl.when(here == 0)
+    def _():
+        meet(ring)
+        ring.start()
+
+    per = (n - 2 + grid_n - 3) // (grid_n - 2)
+
+    @pl.when((here > 0) & (here < grid_n - 1))
+    def _():
+        run_between(ring, jnp.minimum(1 + (here - 1) * per, n - 1), jnp.minimum(1 + here * per, n - 1))
+
+
+def whole_shape(n, shape, kind):
+    rows, cols = shape
+    if kind == "rows":
+        return (n * rows, cols)
+    if kind == "cols":
+        return (rows, n * cols)
+    return (n, rows, cols)
+
+
+ANYWHERE = pl.BlockSpec(memory_space=pl.ANY)
+IN_VMEM = pl.BlockSpec(memory_space=pltpu.VMEM)
+
+
+def comm_params(collective_id):
+    return pltpu.CompilerParams(collective_id=collective_id, has_side_effects=True)
+
+
+class Spread:
+    def __init__(self, axis, n, mine, box, sems):
+        self.axis, self.n, self.mine, self.box = axis, n, mine, box
+        self.send_sem, self.recv_sem = sems
+        self.me = lax.axis_index(axis)
+
+    @staticmethod
+    def scratch(n, shape):
+        dma = pltpu.SemaphoreType.DMA
+        return [pltpu.VMEM((n, *shape), F32), dma((n - 1,)), dma((n - 1,))]
+
+    def greet(self, barrier):
+        def one(off, carry):
+            device = (self.me + off) % self.n
+            pl.semaphore_signal(barrier, inc=1, device_id={self.axis: device}, device_id_type=MESH)
+            return carry
+
+        lax.fori_loop(1, self.n, one, 0)
+        return self.n - 1
+
+    def copy(self, off):
+        return pltpu.make_async_remote_copy(
+            src_ref=self.mine, dst_ref=self.box.at[self.me], send_sem=self.send_sem.at[off - 1],
+            recv_sem=self.recv_sem.at[off - 1], device_id={self.axis: (self.me + off) % self.n}, device_id_type=MESH)
+
+    def arrival(self, off):
+        slot = self.box.at[(self.me + self.n - off) % self.n]
+        return pltpu.make_async_remote_copy(
+            src_ref=self.mine, dst_ref=slot, send_sem=self.send_sem.at[off - 1],
+            recv_sem=self.recv_sem.at[off - 1], device_id={self.axis: (self.me + off) % self.n}, device_id_type=MESH)
+
+    def start(self):
+        def one(off, carry):
+            self.copy(off).start()
+            return carry
+
+        lax.fori_loop(1, self.n, one, 0)
+        self.box[self.me] = self.mine[...]
+
+    def total(self):
+        def one(off, carry):
+            self.arrival(off).wait_recv()
+            self.copy(off).wait_send()
+            return carry
+
+        lax.fori_loop(1, self.n, one, 0)
+        return lax.fori_loop(1, self.n, lambda j, carry: carry + self.box[j], self.box[0])
+
+
+def first_kernel(n, spec, shard_a, shard_b, count_ref, whole_a, whole_b, total_ref, *scratch):
+    ring = RingGather(n, *spec, (shard_a, shard_b), (whole_a, whole_b), scratch[:3])
+    spread = Spread("dp", n, count_ref, scratch[3], scratch[4:])
+    barrier = pltpu.get_barrier_semaphore()
+    pl.semaphore_wait(barrier, spread.greet(barrier))
+    spread.start()
+    ring.start()
+    run_between(ring, 1, n - 1)
+    total_ref[...] = spread.total()
+    ring.finish()
+
+
+def gather_first(packed, gains, count, n):
+    shards = (packed, gains)
+    spec = ([s.shape for s in shards], ("rows", "rows"), (2, 1))
+    return pl.pallas_call(
+        functools.partial(first_kernel, n, spec),
+        in_specs=[ANYWHERE, ANYWHERE, IN_VMEM],
+        out_specs=[ANYWHERE, ANYWHERE, IN_VMEM],
+        out_shape=[jax.ShapeDtypeStruct(whole_shape(n, s.shape, "rows"), BF) for s in shards]
+        + [jax.ShapeDtypeStruct(count.shape, F32)],
+        scratch_shapes=RingGather.scratch(n, spec[0], spec[2]) + Spread.scratch(n, count.shape),
+        compiler_params=comm_params(1),
+    )(packed, gains, count)
+
+
+def rows_of(ref, kind, start, rows):
+    if kind == "cols":
+        return ref.at[pl.ds(start, rows), :]
+    return ref.at[:, pl.ds(start, rows), :]
+
+
+def scatter_gather_kernel(n, spec, start, rows, parts, partial, shard, result, whole, *scratch):
+    quad = QuadScatter(rows, parts, partial, result, scratch[3:])
+    size = spec[0][0][0]
+    ring = RingGather(
+        n, *spec, (shard.at[pl.ds(start, size), :],), (rows_of(whole, spec[1][0], start, size),), scratch[:3])
+    meet(quad, ring)
+    quad.start()
+    ring.start()
+    interleave(ring, quad, n)
+    quad.finish()
+    ring.finish()
+
+
+def scatter_and_gather(partial, shard, kind, start, size, n, collective_id, parts=4):
+    rows, cols = partial.shape[0] // 4, partial.shape[1]
+    spec = ([(size, shard.shape[1])], (kind,), (2,))
+    return pl.pallas_call(
+        functools.partial(scatter_gather_kernel, n, spec, start, rows, parts),
+        in_specs=[ANYWHERE, ANYWHERE],
+        out_specs=[IN_VMEM, ANYWHERE],
+        out_shape=[
+            jax.ShapeDtypeStruct((rows, cols), F32),
+            jax.ShapeDtypeStruct(whole_shape(n, shard.shape, kind), BF),
+        ],
+        scratch_shapes=RingGather.scratch(n, spec[0], spec[2]) + QuadScatter.scratch(rows, cols, parts),
+        compiler_params=comm_params(collective_id),
+    )(partial, shard)
+
+
+def gather_gather_kernel(n, spec, start, rows, parts, mine, shard, _, out, whole, *scratch):
+    quad = QuadGather(rows, parts, mine, out, scratch[3:])
+    size = spec[0][0][0]
+    ring = RingGather(
+        n, *spec, (shard.at[pl.ds(start, size), :],), (rows_of(whole, spec[1][0], start, size),), scratch[:3])
+    meet(quad, ring)
+    quad.start()
+    ring.start()
+    interleave(ring, quad, n)
+    quad.finish()
+    ring.finish()
+
+
+def gather_and_gather(mine, shard, whole, kind, start, size, n, collective_id, parts=4):
+    rows, cols = mine.shape
+    spec = ([(size, shard.shape[1])], (kind,), (2,))
+    return pl.pallas_call(
+        functools.partial(gather_gather_kernel, n, spec, start, rows, parts),
+        in_specs=[ANYWHERE, ANYWHERE, ANYWHERE],
+        out_specs=[ANYWHERE, ANYWHERE],
+        out_shape=[
+            jax.ShapeDtypeStruct((4 * rows, cols), BF),
+            jax.ShapeDtypeStruct(whole.shape, BF),
+        ],
+        input_output_aliases={2: 1},
+        scratch_shapes=RingGather.scratch(n, spec[0], spec[2]) + QuadGather.scratch(parts),
+        compiler_params=comm_params(collective_id),
+    )(mine, shard, whole)
+
+
+def scatter_kernel(rows, parts, partial, result, *scratch):
+    quad = QuadScatter(rows, parts, partial, result, scratch)
+    meet(quad)
+    quad.start()
+    for part in range(parts):
+        quad.step(part)
+    quad.finish()
+
+
+def scatter_rows(partial, collective_id, parts=4):
+    rows, cols = partial.shape[0] // 4, partial.shape[1]
+    return pl.pallas_call(
+        functools.partial(scatter_kernel, rows, parts),
+        in_specs=[ANYWHERE],
+        out_specs=IN_VMEM,
+        out_shape=jax.ShapeDtypeStruct((rows, cols), F32),
+        scratch_shapes=QuadScatter.scratch(rows, cols, parts),
+        compiler_params=comm_params(collective_id),
+    )(partial)
+
+
+def gather_kernel(rows, parts, mine, out, *scratch):
+    quad = QuadGather(rows, parts, mine, out, scratch)
+    meet(quad)
+    quad.start()
+    for part in range(parts):
+        quad.step(part)
+    quad.finish()
+
+
+def gather_rows(mine, collective_id, parts=4):
+    rows, cols = mine.shape
+    return pl.pallas_call(
+        functools.partial(gather_kernel, rows, parts),
+        in_specs=[ANYWHERE],
+        out_specs=ANYWHERE,
+        out_shape=jax.ShapeDtypeStruct((4 * rows, cols), BF),
+        scratch_shapes=QuadGather.scratch(parts),
+        compiler_params=comm_params(collective_id),
+    )(mine)
+
+
+def scatter_scatter_kernel(n, spec, start, rows, parts, partial, grad, result, total, *scratch):
+    count = len(QuadScatter.scratch(rows, 128, parts))
+    quad = QuadScatter(rows, parts, partial, result, scratch[:count])
+    ring = RingScatter(n, *spec, (rows_of(grad, spec[1][0], start, spec[0][0][0]),), (total,), scratch[count:])
+    meet(quad, ring)
+    quad.start()
+    ring.start()
+    interleave(ring, quad, n)
+    quad.finish()
+    ring.finish()
+
+
+def scatter_and_scatter(partial, grad, shape, kind, start, n, collective_id, parts=4):
+    rows, cols = partial.shape[0] // 4, partial.shape[1]
+    spec = ([shape], (kind,), (2,))
+    return pl.pallas_call(
+        functools.partial(scatter_scatter_kernel, n, spec, start, rows, parts),
+        in_specs=[ANYWHERE, ANYWHERE],
+        out_specs=[IN_VMEM, IN_VMEM],
+        out_shape=[jax.ShapeDtypeStruct((rows, cols), F32), jax.ShapeDtypeStruct(shape, F32)],
+        scratch_shapes=QuadScatter.scratch(rows, cols, parts) + RingScatter.scratch(n, spec[0], spec[2]),
+        compiler_params=comm_params(collective_id),
+    )(partial, grad)
+
+
+def gather_scatter_kernel(n, spec, start, rows, parts, mine, grad, out, total, *scratch):
+    count = len(QuadGather.scratch(parts))
+    quad = QuadGather(rows, parts, mine, out, scratch[:count])
+    ring = RingScatter(n, *spec, (rows_of(grad, spec[1][0], start, spec[0][0][0]),), (total,), scratch[count:])
+    meet(quad, ring)
+    quad.start()
+    ring.start()
+    interleave(ring, quad, n)
+    quad.finish()
+    ring.finish()
+
+
+def gather_and_scatter(mine, grad, shape, kind, start, n, collective_id, parts=4):
+    rows, cols = mine.shape
+    spec = ([shape], (kind,), (2,))
+    return pl.pallas_call(
+        functools.partial(gather_scatter_kernel, n, spec, start, rows, parts),
+        in_specs=[ANYWHERE, ANYWHERE],
+        out_specs=[ANYWHERE, IN_VMEM],
+        out_shape=[jax.ShapeDtypeStruct((4 * rows, cols), BF), jax.ShapeDtypeStruct(shape, F32)],
+        scratch_shapes=QuadGather.scratch(parts) + RingScatter.scratch(n, spec[0], spec[2]),
+        compiler_params=comm_params(collective_id),
+    )(mine, grad)
+
+
+def row_sums(weight, grad):
+    ones = jnp.ones((8, weight.shape[1]), F32)
+    return lax.dot_general(
+        ones, weight.astype(F32) * grad, (((1,), (1,)), ((), ())), precision=lax.Precision.HIGHEST,
+        preferred_element_type=F32)
+
+
+def last_kernel(
+    n, spec, rows, parts, misc_at, partial, grad, small, packed, pair, pair_sum, gains,
+    result, total, small_total, misc_total, *scratch,
+):
+    quad_n = len(QuadScatter.scratch(rows, 128, parts))
+    ring_n = len(RingScatter.scratch(n, spec[0], spec[2]))
+    quad = QuadScatter(rows, parts, partial, result, scratch[:quad_n])
+    ring = RingScatter(n, *spec, (grad,), (total,), scratch[quad_n : quad_n + ring_n])
+    rest = scratch[quad_n + ring_n :]
+    wide = Spread("dp", n, small, rest[0], rest[1:3])
+    deep = Spread("tensor", 4, rest[3], rest[4], rest[5:])
+    barrier = pltpu.get_barrier_semaphore()
+    pl.semaphore_wait(barrier, wide.greet(barrier) + deep.greet(barrier))
+    quad.start()
+    ring.start()
+    wide.start()
+    interleave(ring, quad, n)
+    quad.finish()
+    small_total[...] = wide.total()
+    ring.finish()
+    cols = misc_total.shape[1]
+    misc = rest[3]
+    local = packed.shape[0]
+    misc[...] = jnp.zeros_like(misc)
+    misc[0:2, :] = small_total[misc_at : misc_at + 2, 0:cols]
+    gain = gains[0:2, :].astype(F32)
+    misc[2:3, 0:local] = row_sums(packed[...], total[...])[0:1] / gain[0:1]
+    misc[3:4, 0:local] = row_sums(pair[...], pair_sum[...])[0:1] / gain[1:2]
+    deep.start()
+    misc_total[...] = deep.total()
+
+
+def scatter_last(partial, grad, shape, small, misc_at, misc_cols, packed, pair, pair_sum, gains, n, collective_id, parts=4):
+    rows, cols = partial.shape[0] // 4, partial.shape[1]
+    spec = ([shape], ("rows",), (2,))
+    misc_shape = (8, misc_cols)
+    return pl.pallas_call(
+        functools.partial(last_kernel, n, spec, rows, parts, misc_at),
+        in_specs=[ANYWHERE, ANYWHERE] + [IN_VMEM] * 5,
+        out_specs=[IN_VMEM] * 4,
+        out_shape=[
+            jax.ShapeDtypeStruct((rows, cols), F32), jax.ShapeDtypeStruct(shape, F32),
+            jax.ShapeDtypeStruct(small.shape, F32), jax.ShapeDtypeStruct(misc_shape, F32),
+        ],
+        scratch_shapes=QuadScatter.scratch(rows, cols, parts) + RingScatter.scratch(n, spec[0], spec[2])
+        + Spread.scratch(n, small.shape) + [pltpu.VMEM(misc_shape, F32)] + Spread.scratch(4, misc_shape),
+        compiler_params=comm_params(collective_id),
+    )(partial, grad, small, packed, pair, pair_sum, gains)
 
 
 def norm_back(values, rms_inv, gain, d_normed):
     scaled = d_normed * gain
-    gain_grad = jnp.sum(d_normed * values * rms_inv, 0)
-    d_values = rms_inv * scaled - values * rms_inv**3 * jnp.mean(scaled * values, -1, keepdims=True)
-    return (d_values, gain_grad)
+    return rms_inv * scaled - values * rms_inv**3 * jnp.mean(scaled * values, -1, keepdims=True)
 
 
 def weight_grad(source, d_target):
-    return jnp.einsum("td,te->de", source, d_target, preferred_element_type=jnp.float32)
+    return jnp.einsum("td,te->de", source, d_target, preferred_element_type=jnp.float32).astype(BF)
 
 
 def back_product(d_target, weight):
@@ -402,6 +1112,7 @@
     ffn_gain, ffn_gate, ffn_up, ffn_down,
 ):
     seq_count, slot_n, width_n = inputs.shape
+    n = lax.axis_size("dp")
     tokens_n = seq_count * slot_n
     share_n = slot_n // lax.axis_size("tensor")
     share_start = lax.axis_index("tensor") * share_n
@@ -413,102 +1124,108 @@
     wide = 2 * hk + hv
     unit_n = ffn_gate.shape[1]
     local_d = q_weight.shape[0]
+    side = "cols" if local_d % 128 == 0 else "stack"
+
+    def joined(whole):
+        if side == "cols":
+            return whole
+        return whole.transpose(1, 0, 2).reshape(whole.shape[1], -1)
+
+    def parted(grad):
+        if side == "cols":
+            return grad
+        return grad.reshape(grad.shape[0], n, local_d).transpose(1, 0, 2)
 
     positions = lax.broadcasted_iota(jnp.int32, (seq_count, slot_n), 1)
     valid = (positions < lengths[:, None]).astype(jnp.float32)
     tok_weight = valid * loss_mask.astype(jnp.float32)
-    count_all = lax.psum(jnp.sum(tok_weight), "dp")
-
-    spare = BLOCK - 2 * heads - 2
+
     packed = jnp.concatenate(
         [q_weight, k_weight, v_weight, gating_weight, alpha_weight, beta_weight,
-         attn_gain[:, None], ffn_gain[:, None], jnp.zeros((local_d, spare), BF)], 1)
-    proj_w = lax.all_gather(packed, "dp", axis=0, tiled=True)
-    out_w = lax.all_gather(out_weight, "dp", axis=1, tiled=True)
-    pair_w = lax.all_gather(jnp.concatenate([ffn_gate, ffn_up], 1), "dp", axis=0, tiled=True)
-    down_w = lax.all_gather(ffn_down, "dp", axis=1, tiled=True)
-    gain_at = wide + hv + 2 * heads
-    gain_attn = proj_w[:, gain_at].astype(jnp.float32)
-    gain_ffn = proj_w[:, gain_at + 1].astype(jnp.float32)
+         jnp.zeros((local_d, BLOCK - 2 * heads), BF)], 1)
+    pair = jnp.concatenate([ffn_gate, ffn_up], 1)
+    gains = jnp.concatenate([attn_gain[None], ffn_gain[None], jnp.zeros((30, local_d), BF)], 0)
+    proj_w, gains_w, counted = gather_first(packed, gains, jnp.full((8, 128), jnp.sum(tok_weight)), n)
+    count_all = counted[0, 0]
+    gains_w = gains_w.reshape(n, 32, local_d)[:, :2].transpose(1, 0, 2).reshape(2, width_n).astype(jnp.float32)
+    gain_attn, gain_ffn = gains_w[0], gains_w[1]
 
     flat_in = inputs.reshape(tokens_n, width_n).astype(jnp.float32)
     attn_rms = lax.rsqrt(jnp.mean(flat_in * flat_in, -1, keepdims=True) + 1e-06)
     normed = (flat_in * attn_rms * gain_attn).astype(BF)
     proj = jnp.dot(normed, proj_w, preferred_element_type=jnp.float32)
     taps = jnp.pad(jnp.concatenate([q_conv, k_conv, v_conv], 1), ((0, 4), (0, 0)))
-    hp = jnp.zeros((8, BLOCK), jnp.float32).at[0, :heads].set(-jnp.exp(decay_log)).at[1, :heads].set(decay_bias)
-    mixed_low, mix_out, fresh, inverse, states = delta_forward(proj, taps, hp, out_gain[None], heads, dk, dv)
+    hp = jnp.concatenate([-jnp.exp(decay_log)[None], decay_bias[None], jnp.zeros((6, heads), F32)], 0)
+    hp = jnp.pad(hp, ((0, 0), (0, BLOCK - heads)))
+    mixed_low, mix_out, fresh, inverse, states, out_w, pair_w = delta_forward(
+        proj, taps, hp, out_gain[None], (out_weight, pair), (side, "rows"), n, heads, dk, dv)
+    out_w = joined(out_w)
     attn_part = jnp.dot(mixed_low, out_w, preferred_element_type=jnp.float32).astype(BF)
 
     def share_of(array):
         return lax.dynamic_slice_in_dim(array, share_start, share_n, 1)
 
-    def scatter_rows(array):
-        return lax.psum_scatter(array, "tensor", scatter_dimension=0, tiled=True).astype(jnp.float32)
-
-    def gather_rows(array):
-        return lax.all_gather(array, "tensor", axis=0, tiled=True)
-
+    early = unit_n * 6 // 11
+    late = unit_n - early
+    attn_own, down_w = scatter_and_gather(attn_part, ffn_down, side, 0, early, n, 3)
     base_in = share_of(inputs).reshape(share_rows, width_n).astype(jnp.float32)
     base_rms = lax.rsqrt(jnp.mean(base_in * base_in, -1, keepdims=True) + 1e-06)
     row_weight = share_of(tok_weight).reshape(share_rows, 1)
     row_valid = share_of(valid).reshape(share_rows, 1)
     row_teacher = share_of(teacher).reshape(share_rows, width_n).astype(jnp.float32)
-    resid = base_in + scatter_rows(attn_part)
+    resid = base_in + attn_own
     ffn_rms = lax.rsqrt(jnp.mean(resid * resid, -1, keepdims=True) + 1e-06)
-    normed_ffn = gather_rows((resid * ffn_rms * gain_ffn).astype(BF))
+    normed_own = (resid * ffn_rms * gain_ffn).astype(BF)
+    normed_ffn, down_w = gather_and_gather(normed_own, ffn_down, down_w, side, early, late, n, 4)
+    down_w = joined(down_w)
     pre = jnp.dot(normed_ffn, pair_w, preferred_element_type=jnp.float32)
     gate_pre, up_pre = pre[:, :unit_n], pre[:, unit_n:]
     sig_gate = jax.nn.sigmoid(gate_pre)
     silu_gate = gate_pre * sig_gate
     hidden = (silu_gate * up_pre).astype(BF)
     ffn_part = jnp.dot(hidden, down_w, preferred_element_type=jnp.float32).astype(BF)
-    output = resid + scatter_rows(ffn_part)
+    output = resid + scatter_rows(ffn_part, 5)
     error = (output - row_teacher) * row_weight
-    coef = 0.5 * tokens_n * lax.axis_size("dp") / count_all
+    coef = 0.5 * tokens_n * n / count_all
     d_output = 2.0 * coef * error * row_weight
-    d_ffn = gather_rows(d_output.astype(BF))
-    down_grad = weight_grad(hidden, d_ffn).astype(BF)
+    d_ffn = gather_rows(d_output.astype(BF), 6)
+    down_grad = parted(weight_grad(hidden, d_ffn))
     d_hidden = back_product(d_ffn, down_w)
     d_gate = (d_hidden * up_pre * sig_gate * (1.0 + gate_pre * (1.0 - sig_gate))).astype(BF)
     d_up = (d_hidden * silu_gate).astype(BF)
     d_pair = jnp.concatenate([d_gate, d_up], 1)
-    pair_grad = weight_grad(normed_ffn, d_pair).astype(BF)
-    d_nffn = scatter_rows(back_product(d_pair, pair_w).astype(BF))
-    d_resid_norm, ffn_gain_grad = norm_back(resid, ffn_rms, gain_ffn, d_nffn)
-    d_resid = d_output + d_resid_norm
-    d_attn = gather_rows(d_resid.astype(BF))
-    out_grad = weight_grad(mixed_low, d_attn).astype(BF)
+    pair_grad = weight_grad(normed_ffn, d_pair)
+    d_nffn, down_early = scatter_and_scatter(
+        back_product(d_pair, pair_w).astype(BF), down_grad, (early, local_d), side, 0, n, 7)
+    d_resid = d_output + norm_back(resid, ffn_rms, gain_ffn, d_nffn)
+    d_attn, down_late = gather_and_scatter(d_resid.astype(BF), down_grad, (late, local_d), side, early, n, 8)
+    out_grad = parted(weight_grad(mixed_low, d_attn))
     d_mixed = back_product(d_attn, out_w).astype(BF)
-    d_proj, tap_grad, hp_grad, out_gain_part = delta_backward(
-        proj, taps, hp, out_gain[None], mix_out, fresh, inverse, states, d_mixed, heads, dk, dv)
-    proj_grad = weight_grad(normed, d_proj).astype(BF)
-    d_norm = scatter_rows(back_product(d_proj, proj_w).astype(BF))
-    d_in_norm, attn_gain_grad = norm_back(base_in, base_rms, gain_attn, d_norm)
-    input_grad = (d_resid + d_in_norm).reshape(seq_count, share_n, width_n)
+    d_proj, tap_grad, hp_grad, out_gain_part, out_sum, pair_sum = delta_backward(
+        proj, taps, hp, out_gain[None], mix_out, fresh, inverse, states, d_mixed,
+        (out_grad, pair_grad), (out_weight.shape, pair.shape), (side, "rows"), n, heads, dk, dv)
+    proj_grad = weight_grad(normed, d_proj)
+    d_norm_part = back_product(d_proj, proj_w).astype(BF)
+
+    def line(values):
+        return jnp.pad(values, ((0, 0), (0, wide - values.shape[1])))
+
+    small = jnp.concatenate(
+        [tap_grad[:4], line(hp_grad[:2]), line(out_gain_part), jnp.full((1, wide), jnp.sum(error * error))], 0)
+    misc_cols = max(dv, -(-local_d // 128) * 128)
+    d_norm, proj_sum, small_sum, misc_sum = scatter_last(
+        d_norm_part, proj_grad, packed.shape, small, 6, misc_cols, packed, pair, pair_sum, gains, n, 10)
+    input_grad = (d_resid + norm_back(base_in, base_rms, gain_attn, d_norm)).reshape(seq_count, share_n, width_n)
     activations = (output * row_valid).astype(BF).reshape(seq_count, share_n, width_n)
-
-    down_sum = lax.psum_scatter(down_grad, "dp", scatter_dimension=1, tiled=True).astype(jnp.float32)
-    pair_sum = lax.psum_scatter(pair_grad, "dp", scatter_dimension=0, tiled=True).astype(jnp.float32)
-    out_sum = lax.psum_scatter(out_grad, "dp", scatter_dimension=1, tiled=True).astype(jnp.float32)
-    proj_sum = lax.psum_scatter(proj_grad, "dp", scatter_dimension=0, tiled=True).astype(jnp.float32)
-
-    error_all, gains_all, out_gain_sum = lax.psum(
-        (jnp.sum(error * error), jnp.concatenate([attn_gain_grad, ffn_gain_grad]), out_gain_part[0]), ("dp", "tensor"))
-    loss = error_all / count_all
-    gain_len = width_n // lax.axis_size("dp")
-    gain_start = lax.axis_index("dp") * gain_len
-    attn_gain_out = lax.dynamic_slice_in_dim(gains_all, gain_start, gain_len, 0)
-    ffn_gain_out = lax.dynamic_slice_in_dim(gains_all, width_n + gain_start, gain_len, 0)
-    small = jnp.concatenate([tap_grad[:4], jnp.pad(hp_grad[:4], ((0, 0), (0, 0)))], 1)
-    small = lax.psum(small, "dp")
+    loss = misc_sum[1, 0] / count_all
     return (
-        activations, loss, input_grad, attn_gain_out,
+        activations, loss, input_grad, misc_sum[2, :local_d],
         proj_sum[:, :hk], proj_sum[:, hk : 2 * hk], proj_sum[:, 2 * hk : wide], proj_sum[:, wide : wide + hv],
         proj_sum[:, wide + hv : wide + hv + heads], proj_sum[:, wide + hv + heads : wide + hv + 2 * heads],
-        small[:, :hk], small[:, hk : 2 * hk], small[:, 2 * hk : wide],
-        small[0, wide : wide + heads], small[1, wide : wide + heads], out_gain_sum,
-        out_sum, ffn_gain_out, pair_sum[:, :unit_n], pair_sum[:, unit_n:], down_sum,
+        small_sum[:4, :hk], small_sum[:4, hk : 2 * hk], small_sum[:4, 2 * hk : wide],
+        small_sum[4, :heads], small_sum[5, :heads], misc_sum[0, :dv],
+        out_sum, misc_sum[3, :local_d], pair_sum[:, :unit_n], pair_sum[:, unit_n:],
+        jnp.concatenate([down_early, down_late], 0),
     )
 
 

time: 1560 us -> 1050 us (0.67)
  waiting for transfers between devices: 1050 us -> 0 us
  Pallas kernels: 141 us -> 810 us
  blocking collectives: 96.2 us -> 0 us
    pallas_call x2 -> x10, Pallas kernels: 141 us -> 810 us  [the longest x1 155 us: delta_forward(): pl.pallas_call(functools.partial(forward_kernel, heads, dk, dv, n, steps,...]
    reduce_scatter x8 -> x0, waiting for transfers between devices: 543 us -> none  [the longest x1 211 us: body(): lax.psum_scatter(proj_grad, 'dp', scatter_dimension=0, tiled=True)]
    all_gather x7 -> x0, waiting for transfers between devices: 507 us -> none  [the longest x1 181 us: body(): proj_w = lax.all_gather(packed, 'dp', axis=0, tiled=True)]
    psum x3 -> x0, blocking collectives: 96.2 us -> none  [the longest x1 39.4 us: body(): lax.psum((jnp.sum(error * error), jnp.concatenate([attn_gain_grad, ffn_ga...]
  transfers between devices with their start and end apart: 15 -> 0, of which waited for: 12 -> 0; matrix products, arithmetic and copies ran while one was open for 10% -> 0% of each run, Pallas kernels for 9% -> 0%
where the time goes in v2:
time: 1050 us; the launch traced here: 1040 us
  Pallas kernels  810 us (77%)
  matrix products  170 us (16%)
  other arithmetic  30.8 us (3%)
  local copies, waits for them, and re-layouts  27.7 us (3%)
    pallas_call x1, Pallas kernels, delta_forward(): pl.pallas_call(functools.partial(forward_kernel, heads, dk, dv, n, steps,...  155 us
    pallas_call x1, Pallas kernels, delta_backward(): pl.pallas_call(functools.partial(backward_kernel, heads, dk, dv, n, steps...  153 us
    pallas_call x1, Pallas kernels, scatter_last(): pl.pallas_call(functools.partial(last_kernel, n, spec, rows, parts, misc_...  148 us
    pallas_call x1, Pallas kernels, gather_first(): pl.pallas_call(functools.partial(first_kernel, n, spec), in_specs=[ANYWHE...  134 us
    dot_general x4, matrix products, back_product(): jnp.einsum('te,de->td', d_target, weight, preferred_element_type=jnp.floa...  62.5 us
    dot_general x4, matrix products, weight_grad(): jnp.einsum('td,te->de', source, d_target, preferred_element_type=jnp.floa...  49.2 us
    pallas_call x1, Pallas kernels, gather_and_gather(): pl.pallas_call(functools.partial(gather_gather_kernel, n, spec, start, ro...  45.2 us
    pallas_call x1, Pallas kernels, gather_and_scatter(): pl.pallas_call(functools.partial(gather_scatter_kernel, n, spec, start, r...  38.6 us

profile of v2, /device:TPU:0, one launch (start us, length us, event | category | flops | bytes accessed | tf_op | source)
XLA Modules:
  0.0 1044.0 jit_solution(10797671298019476680)
XLA Ops:
  1.6 0.7 negate_bitcast_fusion
  2.4 0.7 broadcast_in_dim.33
  3.1 0.7 broadcast_in_dim.34
  3.7 0.7 maximum_maximum_fusion.1
  4.4 0.6 pad.17.hp_ref
  5.0 3.1 fusion
  8.3 0.6 fusion.23
  8.9 1.2 broadcast_in_dim.36.count_ref
  10.1 0.7 maximum_maximum_fusion.shard_b.gains
  10.8 0.6 select_maximum_fusion.2.taps_ref
  11.8 2.0 concatenate.24.shard_a.packed
  13.9 134.0 %shard_map.373 = (bf16[2048,3200]{1,0:T(8,128)(2,1)}, bf16[256,256]{1,0:T(8,128)(2,1)}, f32[8,128]{1,0:T(8,128)}) custom-call(bf16[256,3200]{1,0:T(8,128)(2,1)} %concatenate.24.shard_a.packed, bf16[32,256]{1,0:T(8,128)(2,1)} %maximum_maximum_fusion.shard_b.gains, f32[8,128]{1,0:T(8,128)} %broadcast_in_dim.36.count_ref), custom_call_target="tpu_custom_call" | custom-call | tf_op jit(solution)/shard_map/pallas_call | solution.py:871
  147.9 1.2 slice.82
  149.8 0.8 convert_bitcast_fusion
  150.6 22.9 %fusion.13.proj_ref.halo_ref = f32[1024,3200]{1,0:T(8,128)} fusion(bf16[2048,3200]{1,0:T(8,128)(2,1)} %get-tuple-element.50, bf16[1,1024,2048]{2,1,0:T(8,128)(2,1)} %param.22, f32[2048]{0:T(1024)S(1)} %bitcast.68, f32[1024]{0:T(1024)S(1)} %add_rsqrt_fusion), kind=kOutput, calls=%fused_computation.41 | convolution fusion | flops 13430161408 | bytes 30420992 | tf_op jit(solution)/shard_map/dot_general | solution.py:1156
  173.5 154.8 %shard_map.374 = (bf16[1024,1024]{1,0:T(8,128)(2,1)}, bf16[1024,1024]{1,0:T(8,128)(2,1)}, bf16[1024,1024]{1,0:T(8,128)(2,1)}, bf16[1024,512]{1,0:T(8,128)(2,1)},...) custom-call(f32[1024,3200]{1,0:T(8,128)} %fusion.13.proj_ref.halo_ref, ...), custom_call_target="tpu_custom_call" | custom-call | flops 4026531840 | bytes 30720000 | tf_op jit(solution)/shard_map/pallas_call | solution.py:173
  328.3 9.3 convolution_convert_fusion.7.partial
  337.6 37.0 %shard_map.375 = (f32[256,2048]{1,0:T(8,128)}, bf16[1408,2048]{1,0:T(8,128)(2,1)}) custom-call(bf16[1024,2048]{1,0:T(8,128)(2,1)} %convolution_convert_fusion.7.partial, bf16[1408,256]{1,0:T(8,128)(2,1)} %shard.3), custom_call_target="tpu_custom_call" | custom-call | tf_op jit(solution)/shard_map/pallas_call | solution.py:904
  374.6 2.2 multiply_reduce_fusion.2
  376.9 1.2 multiply_convert_fusion.4.mine
  378.1 45.2 %shard_map.376 = (bf16[1024,2048]{1,0:T(8,128)(2,1)}, bf16[1408,2048]{1,0:T(8,128)(2,1)}) custom-call(bf16[256,2048]{1,0:T(8,128)(2,1)} %multiply_convert_fusion.4.mine, bf16[1408,256]{1,0:T(8,128)(2,1)} %shard.3, bf16[1408,2048]{1,0:T(8,128)(2,1)} %get-tuple-element.54._), custom_call_target="tpu_custom_call", output_to_operand_aliasing={{1}: (2, {})} | custom-call | tf_op jit(solution)/shard_map/pallas_call | solution.py:933
  423.3 17.2 %fusion.31 = f32[1024,2816]{1,0:T(8,128)S(1)} fusion(bf16[1024,2048]{1,0:T(8,128)(2,1)} %get-tuple-element.55, bf16[2048,2816]{1,0:T(8,128)(2,1)} %get-tuple-element.56), kind=kOutput, calls=%fused_computation.85 | convolution fusion | flops 11811160064 | bytes 27262976 | tf_op jit(solution)/shard_map/dot_general | solution.py:1181
  440.5 1.8 multiply_convert_fusion.2
  442.4 4.0 copy-done.4
  446.4 1.6 copy-done.11
  447.9 8.6 convolution_convert_fusion.5.partial
  456.6 28.7 %shard_map.377 = f32[256,2048]{1,0:T(8,128)} custom-call(bf16[1024,2048]{1,0:T(8,128)(2,1)} %convolution_convert_fusion.5.partial), custom_call_target="tpu_custom_call" | custom-call | tf_op jit(solution)/shard_map/pallas_call | solution.py:958
  485.3 4.4 multiply_reduce_fusion
  489.7 0.7 pad.25.clone
  490.4 0.6 copy-done
  491.0 1.2 fusion.11.mine
  492.2 34.3 %shard_map.378 = bf16[1024,2048]{1,0:T(8,128)(2,1)} custom-call(bf16[256,2048]{1,0:T(8,128)(2,1)} %fusion.11.mine), custom_call_target="tpu_custom_call" | custom-call | tf_op jit(solution)/shard_map/pallas_call | solution.py:979
  526.5 15.3 %multiply_convert_fusion.1 = (bf16[1024,1408]{1,0:T(8,128)(2,1)S(1)}, bf16[1024,1408]{1,0:T(8,128)(2,1)}) fusion(f32[1024,2816]{1,0:T(8,128)} %copy-done.4, bf16[1024,2048]{1,0:T(8,128)(2,1)} %shard_map.378, bf16[1408,2048]{1,0:T(8,128)(2,1)} %get-tuple-element.57), kind=kOutput, calls=%fused_computation.10 | convolution fusion | flops 5924323328 | bytes 27262976 | tf_op jit(solution)/shard_map/te,de->td/dot_general | solution.py:1106
  541.8 8.1 convolution_convert_fusion.2.grad
  549.9 17.4 %convolution_convert_fusion.4.partial = bf16[1024,2048]{1,0:T(8,128)(2,1)} fusion(bf16[2048,2816]{1,0:T(8,128)(2,1)} %get-tuple-element.56, bf16[1024,1408]{1,0:T(8,128)(2,1)} %get-tuple-element.109, bf16[1024,1408]{1,0:T(8,128)(2,1)S(1)} %get-tuple-element.108), kind=kOutput, calls=%fused_computation.15 | convolution fusion | flops 11824791552 | bytes 21495808 | tf_op jit(solution)/shard_map/te,de->td/dot_general | solution.py:1106
  567.3 36.5 %shard_map.379 = (f32[256,2048]{1,0:T(8,128)}, f32[768,256]{1,0:T(8,128)}) custom-call(bf16[1024,2048]{1,0:T(8,128)(2,1)} %convolution_convert_fusion.4.partial, bf16[1408,2048]{1,0:T(8,128)(2,1)} %convolution_convert_fusion.2.grad), custom_call_target="tpu_custom_call" | custom-call | tf_op jit(solution)/shard_map/pallas_call | solution.py:1004
  603.8 2.0 multiply_reduce_fusion.1
  605.9 0.2 copy-done.1
  606.0 0.6 copy-done.6
  606.7 2.5 fusion.22
  609.1 38.6 %shard_map.380 = (bf16[1024,2048]{1,0:T(8,128)(2,1)}, f32[640,256]{1,0:T(8,128)}) custom-call(bf16[256,2048]{1,0:T(8,128)(2,1)} %get-tuple-element.102.mine, bf16[1408,2048]{1,0:T(8,128)(2,1)} %convolution_convert_fusion.2.grad), custom_call_target="tpu_custom_call" | custom-call | tf_op jit(solution)/shard_map/pallas_call | solution.py:1029
  647.8 9.5 convolution_convert_fusion.8.dm_ref
  657.3 1.2 pad_maximum_fusion.3
  658.5 16.8 %convolution_convert_fusion.1.grad_b = bf16[2048,2816]{1,0:T(8,128)(2,1)} fusion(bf16[1024,2048]{1,0:T(8,128)(2,1)S(1)} %copy-done.35, bf16[1024,1408]{1,0:T(8,128)(2,1)} %get-tuple-element.109, bf16[1024,1408]{1,0:T(8,128)(2,1)S(1)} %copy-done.39), kind=kOutput, calls=%fused_computation.1 | convolution fusion | flops 11828461568 | bytes 21495808 | tf_op jit(solution)/shard_map/td,te->de/dot_general | solution.py:1102
  675.3 6.2 convolution_convert_fusion.6.grad_a
  681.5 152.6 %shard_map.381 = (bf16[1024,3200]{1,0:T(8,128)(2,1)}, f32[8,2048]{1,0:T(8,128)}, f32[8,128]{1,0:T(8,128)}, f32[1,256]{1,0:T(1,128)}, f32[1024,256]{1,0:T(8,128)}, /*index=5*/f32[256,2816]{1,0:T(8,128)}) custom-call(f32[1024,3200]{1,0:T(8,128)} %fusion.13.proj_ref.halo_ref, f32[1024,3200]{1,0:T(8,128)} %fusion.13.proj_ref.halo_ref, ...), custom_call_target="tpu_custom_call" | custom-call | flops 6442450944 | bytes 40960000 | tf_op jit(solution)/shard_map/pallas_call | solution.py:375
  834.1 20.4 %convolution_convert_fusion.3.partial = bf16[1024,2048]{1,0:T(8,128)(2,1)} fusion(bf16[1024,3200]{1,0:T(8,128)(2,1)} %get-tuple-element.65, bf16[2048,3200]{1,0:T(8,128)(2,1)} %get-tuple-element.50), kind=kOutput, calls=%fused_computation.14 | convolution fusion | flops 13423869952 | bytes 23855104 | tf_op jit(solution)/shard_map/te,de->td/dot_general | solution.py:1106
  854.5 0.8 slice.84
  855.4 0.7 fusion.16.small
  856.1 1.8 fusion.27
  857.9 18.1 %convolution_convert_fusion.grad = bf16[2048,3200]{1,0:T(8,128)(2,1)} fusion(bf16[1024,3200]{1,0:T(8,128)(2,1)S(1)} %bitcast.84, bf16[1,1024,2048]{2,1,0:T(8,128)(2,1)S(1)} %copy-done.2, f32[2048]{0:T(1024)S(1)} %bitcast.69, f32[1024]{0:T(1024)S(1)} %copy-done.31), kind=kOutput, calls=%fused_computation | convolution fusion | flops 13436715008 | bytes 23867392 | tf_op jit(solution)/shard_map/td,te->de/dot_general | solution.py:1102
  876.0 148.3 %shard_map.382 = (f32[256,2048]{1,0:T(8,128)}, f32[256,3200]{1,0:T(8,128)}, f32[8,2048]{1,0:T(8,128)}, f32[8,256]{1,0:T(8,128)}) custom-call(bf16[1024,2048]{1,0:T(8,128)(2,1)} %convolution_convert_fusion.3.partial, bf16[2048,3200]{1,0:T(8,128)(2,1)} %convolution_convert_fusion.grad, f32[8,2048]{1,0:T(8,128)} %fusion.16.small, ...), custom_call_target="tpu_custom_call" | custom-call | tf_op jit(solution)/shard_map/pallas_call | solution.py:1082
  1024.4 1.3 slice.85
  1027.1 1.4 fusion.30
  1028.4 1.3 slice_bitcast_fusion
  1029.7 2.4 fusion.4
  1032.2 3.9 fusion.8
  1036.1 0.6 slice.95
  1036.7 0.6 fusion.28
  1037.4 0.7 copy.47
  1038.1 0.7 copy.46
  1038.8 1.1 fusion.26
  1039.9 1.6 fusion.25
  1041.5 1.0 copy.52
  (99 shorter events, 0.9 us)
Async XLA Ops:
  0.7 13.1 %copy-start.15 = (bf16[256,1408]{1,0:T(8,128)(2,1)S(1)}, bf16[256,1408]{1,0:T(8,128)(2,1)}, u32[]{:S(2)}) copy-start(bf16[256,1408]{1,0:T(8,128)(2,1)} %param.41) | copy-start | bytes 2162692
  0.7 10.1 copy-start.26
  0.7 10.1 copy-start.27
  0.7 10.1 copy-start.28
  0.7 10.9 %copy-start.33 = (bf16[256,4]{0,1:T(4,128)(2,1)S(1)}, bf16[256,4]{0,1:T(4,128)(2,1)}, u32[]{:S(2)}) copy-start(bf16[256,4]{0,1:T(4,128)(2,1)} %param.32) | copy-start | bytes 6148
  0.7 10.7 %copy-start.32 = (bf16[256,4]{0,1:T(4,128)(2,1)S(1)}, bf16[256,4]{0,1:T(4,128)(2,1)}, u32[]{:S(2)}) copy-start(bf16[256,4]{0,1:T(4,128)(2,1)} %param.31) | copy-start | bytes 6148
  0.7 11.0 %copy-start.19 = (bf16[256,1024]{1,0:T(8,128)(2,1)S(1)}, bf16[256,1024]{1,0:T(8,128)(2,1)}, u32[]{:S(2)}) copy-start(bf16[256,1024]{1,0:T(8,128)(2,1)} %param.30) | copy-start | bytes 1572868
  0.7 11.0 %copy-start.18 = (bf16[256,1024]{1,0:T(8,128)(2,1)S(1)}, bf16[256,1024]{1,0:T(8,128)(2,1)}, u32[]{:S(2)}) copy-start(bf16[256,1024]{1,0:T(8,128)(2,1)} %param.29) | copy-start | bytes 1572868
  0.7 11.0 %copy-start.21 = (bf16[256,512]{1,0:T(8,128)(2,1)S(1)}, bf16[256,512]{1,0:T(8,128)(2,1)}, u32[]{:S(2)}) copy-start(bf16[256,512]{1,0:T(8,128)(2,1)} %param.28) | copy-start | bytes 786436
  0.8 11.0 %copy-start.20 = (bf16[256,512]{1,0:T(8,128)(2,1)S(1)}, bf16[256,512]{1,0:T(8,128)(2,1)}, u32[]{:S(2)}) copy-start(bf16[256,512]{1,0:T(8,128)(2,1)} %param.27) | copy-start | bytes 786436
  0.8 7.5 copy-start.29
  5.0 8.8 copy-start.16
  8.2 165.3 %copy-start.30 = (f32[1024]{0:T(1024)}, f32[1024]{0:T(1024)S(1)}, u32[]{:S(2)}) copy-start(f32[1024]{0:T(1024)S(1)} %add_rsqrt_fusion) | copy-start | bytes 12292
  13.9 159.6 %copy-start.5 = (bf16[256,2816]{1,0:T(8,128)(2,1)}, bf16[256,2816]{1,0:T(8,128)(2,1)S(1)}, u32[]{:S(2)}) copy-start(bf16[256,2816]{1,0:T(8,128)(2,1)S(1)} %constant_dynamic-update-slice_fusion.shard_b.pair) | copy-start | bytes 4325380
  150.6 22.9 %copy-start.22 = (f32[1,8,256]{2,0,1:T(1,128)}, f32[1,8,256]{2,0,1:T(1,128)S(1)}, u32[]{:S(2)}) copy-start(f32[1,8,256]{2,0,1:T(1,128)S(1)} %get-tuple-element.124) | copy-start | bytes 24580
  440.5 5.8 copy-start.4
  440.5 7.4 copy-start.8
  446.4 1.6 copy-start.11
  489.7 1.3 copy-start
  526.5 15.3 %copy-start.9 = (bf16[1024,2048]{1,0:T(8,128)(2,1)S(1)}, bf16[1024,2048]{1,0:T(8,128)(2,1)}, u32[]{:S(2)}) copy-start(bf16[1024,2048]{1,0:T(8,128)(2,1)} %shard_map.378) | copy-start | bytes 12582916
  526.5 15.3 %copy-start.12 = (bf16[1024,1408]{1,0:T(8,128)(2,1)S(1)}, bf16[1024,1408]{1,0:T(8,128)(2,1)}, u32[]{:S(2)}) copy-start(bf16[1024,1408]{1,0:T(8,128)(2,1)} %copy-done.11) | copy-start | bytes 8650756
  541.8 8.1 copy-start.38
  603.8 2.2 copy-start.1
  603.8 2.8 copy-start.6
  647.8 9.5 copy-start.14
  647.8 9.5 copy-start.17
  647.8 10.7 %copy-start.35 = (bf16[1024,2048]{1,0:T(8,128)(2,1)S(1)}, bf16[1024,2048]{1,0:T(8,128)(2,1)}, u32[]{:S(2)}) copy-start(bf16[1024,2048]{1,0:T(8,128)(2,1)} %get-tuple-element.55) | copy-start | bytes 12582916
  647.8 10.7 %copy-start.39 = (bf16[1024,1408]{1,0:T(8,128)(2,1)S(1)}, bf16[1024,1408]{1,0:T(8,128)(2,1)}, u32[]{:S(2)}) copy-start(bf16[1024,1408]{1,0:T(8,128)(2,1)} %copy-done.38) | copy-start | bytes 8650756
  658.5 16.8 %copy-start.36 = (bf16[1024,2048]{1,0:T(8,128)(2,1)S(1)}, bf16[1024,2048]{1,0:T(8,128)(2,1)}, u32[]{:S(2)}) copy-start(bf16[1024,2048]{1,0:T(8,128)(2,1)} %get-tuple-element.64) | copy-start | bytes 12582916
  658.5 16.8 %copy-start.37 = (bf16[1024,1024]{1,0:T(8,128)(2,1)S(1)}, bf16[1024,1024]{1,0:T(8,128)(2,1)}, u32[]{:S(2)}) copy-start(bf16[1024,1024]{1,0:T(8,128)(2,1)} %get-tuple-element.51) | copy-start | bytes 6291460
  834.1 23.8 %slice-start = ((s8[6553600]{0:T(1024)(128)(4,1)}), s8[4194304]{0:T(1024)(128)(4,1)S(1)}, s32[]{:S(2)}) async-start(s8[6553600]{0:T(1024)(128)(4,1)} %bitcast.83), calls=%async_computation | async-start | bytes 8388608
  834.1 20.4 %copy-start.25 = (f32[8,2048]{1,0:T(8,128)S(1)}, f32[8,2048]{1,0:T(8,128)}, u32[]{:S(2)}) copy-start(f32[8,2048]{1,0:T(8,128)} %get-tuple-element.66) | copy-start | bytes 196612
  834.1 21.3 %copy-start.34 = (f32[1,256]{1,0:T(1,128)S(1)}, f32[1,256]{1,0:T(1,128)}, u32[]{:S(2)}) copy-start(f32[1,256]{1,0:T(1,128)} %get-tuple-element.68) | copy-start | bytes 3076
  834.1 22.0 %copy-start.3 = (f32[256,2816]{1,0:T(8,128)S(1)}, f32[256,2816]{1,0:T(8,128)}, u32[]{:S(2)}) copy-start(f32[256,2816]{1,0:T(8,128)} %get-tuple-element.69.pair_sum) | copy-start | bytes 8650756
  834.1 23.7 %slice-start.1 = ((s8[6553600]{0:T(1024)(128)(4,1)}), s8[2359296]{0:T(1024)(128)(4,1)S(1)}, s32[]{:S(2)}) async-start(s8[6553600]{0:T(1024)(128)(4,1)} %bitcast.83), calls=%async_computation.1 | async-start | bytes 4718592
  854.5 3.3 copy-start.2
  854.5 3.3 copy-start.23
  854.5 3.4 copy-start.31
  1024.4 7.8 copy-start.7
  1032.1 4.0 copy-start.24
  1032.1 5.2 copy-start.10
  1038.8 2.7 copy-start.13
